TPU v7x, 256 devices: a whole 4x4x8 slice. The times are simulated.
256 devices in a mesh: chan: 16 (over z, y_lo), tm: 16 (over x, y_hi, core).
Axes of the slice: x: 4, y: 4 (y_hi: 2, y_lo: 2; y = y_hi * 2 + y_lo), z: 8, core: 2. Of those that a mesh axis runs over, the one named last changes fastest.
Arguments:
- raw: float32 [2, 512, 4096], P(None, 'chan', 'tm'), may hold values from -40 to 40
- alive: int32 [512], P(('chan', 'tm')), may hold values 0 or 1
- seg_start: int32 [2], replicated, may hold values from 0 to 256, as said below
- norm_half: int32 [512], P(('chan', 'tm')), may hold values from 32 to 64, as said below
Outputs:
- corr: bfloat16 [512, 129, 512], P(('chan', 'tm'))
Inputs may be any that keep to these rules, and one draw needn't show every extreme that they name: `seg_start`: some segment starts exactly 256 samples into its window. `norm_half`: some channel has half-length 32 and some 64.
All inputs are finite; a program needn't handle non-finite values. No bound on the sum of `alive` on one device may be relied on, other than what follows from the above.
Results may differ from a plain program's by a relative error of at most 0.02.
Values may be sent and summed in bfloat16 or wider, within the bound.
No kernel may reach another device: no remote copies, remote signals or barrier semaphores. Data moves between devices by JAX's collectives and lax.ppermute only.
A program may use at most 64 MiB of HBM per device.

v0:
```python
import math

import jax
import jax.numpy as jnp
from jax import lax
from jax.sharding import PartitionSpec as P

LAG = 64


widest = 64
smooth_half = 32
tiny = 1e-05
radix = 128


def shifted(value, axis, by):
    length = lax.axis_size(axis)
    return lax.ppermute(value, axis, [(i, (i + by) % length) for i in range(length)])


def window_mean(signal, half_width):
    length = signal.shape[2]
    padded = jnp.pad(jnp.abs(signal), ((0, 0), (0, 0), (widest, widest)))
    running = jnp.cumsum(padded, axis=2)
    running = jnp.concatenate([jnp.zeros(running.shape[:2] + (1,), jnp.float32), running], axis=2)
    moments = jnp.arange(length, dtype=jnp.int32)
    full_shape = signal.shape
    upper_index = jnp.broadcast_to(
        moments[None, None, :] + half_width[None, :, None] + 1 + widest, full_shape
    )
    lower_index = jnp.broadcast_to(
        moments[None, None, :] - half_width[None, :, None] + widest, full_shape
    )
    total = jnp.take_along_axis(running, upper_index, axis=2) - jnp.take_along_axis(
        running, lower_index, axis=2
    )
    return total / (2 * half_width[None, :, None] + 1).astype(jnp.float32)


def phase_table(row_total, col_total, modulus):
    product = (
        jnp.arange(row_total, dtype=jnp.int32)[:, None]
        * jnp.arange(col_total, dtype=jnp.int32)[None, :]
        % modulus
    )
    angle = product.astype(jnp.float32) * (2.0 * math.pi / modulus)
    return (jnp.cos(angle), jnp.sin(angle))


def forward_transform(signal, cos_q, sin_q, cos_p, sin_p, cos_t, sin_t):
    length = signal.shape[1]
    inner = length // radix
    highest = lax.Precision.HIGHEST
    grid = signal.reshape(-1, inner, radix)
    first_re = jnp.einsum("rqp,qk->rkp", grid, cos_q, precision=highest)
    first_im = -jnp.einsum("rqp,qk->rkp", grid, sin_q, precision=highest)
    turned_re = first_re * cos_t + first_im * sin_t
    turned_im = first_im * cos_t - first_re * sin_t
    out_re = jnp.einsum("rkp,pj->rjk", turned_re, cos_p, precision=highest) + jnp.einsum(
        "rkp,pj->rjk", turned_im, sin_p, precision=highest
    )
    out_im = jnp.einsum("rkp,pj->rjk", turned_im, cos_p, precision=highest) - jnp.einsum(
        "rkp,pj->rjk", turned_re, sin_p, precision=highest
    )
    return (out_re.reshape(-1, length), out_im.reshape(-1, length))


def inverse_real(spec_re, spec_im, cos_q, sin_q, cos_p, sin_p, cos_t, sin_t):
    length = spec_re.shape[1]
    inner = length // radix
    highest = lax.Precision.HIGHEST
    grid_re = spec_re.reshape(-1, radix, inner)
    grid_im = spec_im.reshape(-1, radix, inner)
    first_re = jnp.einsum("rjk,jp->rkp", grid_re, cos_p, precision=highest) - jnp.einsum(
        "rjk,jp->rkp", grid_im, sin_p, precision=highest
    )
    first_im = jnp.einsum("rjk,jp->rkp", grid_im, cos_p, precision=highest) + jnp.einsum(
        "rjk,jp->rkp", grid_re, sin_p, precision=highest
    )
    turned_re = first_re * cos_t - first_im * sin_t
    turned_im = first_im * cos_t + first_re * sin_t
    result = jnp.einsum("rkp,kq->rqp", turned_re, cos_q, precision=highest) - jnp.einsum(
        "rkp,kq->rqp", turned_im, sin_q, precision=highest
    )
    return result.reshape(-1, length)


def whiten(normed):
    segs, rows, length = normed.shape
    inner = length // radix
    cos_q, sin_q = phase_table(inner, inner, inner)
    cos_p, sin_p = phase_table(radix, radix, radix)
    cos_t, sin_t = phase_table(inner, radix, length)
    spec_re, spec_im = forward_transform(
        normed.reshape(-1, length), cos_q, sin_q, cos_p, sin_p, cos_t, sin_t
    )
    magnitude = jnp.sqrt(spec_re * spec_re + spec_im * spec_im)
    circular = jnp.concatenate(
        [magnitude[:, length - smooth_half :], magnitude, magnitude[:, :smooth_half]], axis=1
    )
    running = jnp.cumsum(circular, axis=1)
    running = jnp.concatenate([jnp.zeros((running.shape[0], 1), jnp.float32), running], axis=1)
    span_bins = 2 * smooth_half + 1
    smooth = (running[:, span_bins:] - running[:, :-span_bins]) / span_bins
    bins = jnp.arange(length, dtype=jnp.int32)
    folded = jnp.minimum(bins, length - bins)
    band = ((folded >= length // 250) & (folded <= 2 * length // 5)).astype(jnp.float32)
    gain = band[None, :] / (smooth + tiny)
    traces = inverse_real(spec_re * gain, spec_im * gain, cos_q, sin_q, cos_p, sin_p, cos_t, sin_t)
    return (traces * (1.0 / math.sqrt(length))).reshape(segs, rows, length).astype(jnp.bfloat16)


def lag_ranges(lag_count):
    block_size = -(-lag_count // 3)
    return [
        (block_first, min(block_first + block_size, lag_count))
        for block_first in range(0, lag_count, block_size)
    ]


def on_device(raw, alive, seg_start, norm_half):
    segs, width, span = raw.shape
    groups = lax.axis_size("tm")
    chan_count = lax.axis_size("chan")
    rows = alive.shape[0]
    length = span * groups
    channel_total = width * chan_count
    lag_count = 2 * LAG + 1
    chan_index = lax.axis_index("chan")
    time_index = lax.axis_index("tm")
    gathered = lax.all_to_all(raw, "tm", split_axis=1, concat_axis=2, tiled=True)
    gathered = gathered * alive.astype(jnp.float32)[None, :, None]
    pieces = []
    for segment in range(segs):
        padded = jnp.pad(gathered[segment], ((0, 0), (0, length)))
        pieces.append(lax.dynamic_slice_in_dim(padded, seg_start[segment], length, axis=1))
    signal = jnp.stack(pieces, axis=0)
    level = window_mean(signal, norm_half)
    normed = signal / (level + tiny)
    white = whiten(normed)
    row_ids = (chan_index * groups + time_index) * rows + jnp.arange(rows, dtype=jnp.int32)
    col_ids = jnp.arange(channel_total, dtype=jnp.int32)
    keep = row_ids[:, None, None] != col_ids[None, None, :]
    collected = jnp.zeros((rows, lag_count, channel_total), jnp.float32)
    padded_white = jnp.pad(white, ((0, 0), (0, 0), (LAG, span)))
    before = padded_white[:, :, :length].reshape(segs, rows, groups, span)[..., :LAG]
    after = padded_white[:, :, span + LAG : span + LAG + length].reshape(segs, rows, groups, span)[
        ..., :LAG
    ]
    framed_pieces = jnp.concatenate(
        [before, white.reshape(segs, rows, groups, span), after], axis=3
    )
    framed = lax.all_to_all(framed_pieces, "tm", split_axis=2, concat_axis=1, tiled=True).reshape(
        segs, width, span + 2 * LAG
    )
    own_slab = framed[:, :, LAG : LAG + span]

    def slab_block(partner):
        parts = []
        for block_first, block_last in lag_ranges(lag_count):
            stacked = jnp.stack(
                [
                    partner[:, :, offset : offset + span]
                    for offset in range(block_first, block_last)
                ],
                axis=1,
            )
            parts.append(
                jnp.einsum("sit,sljt->ilj", own_slab, stacked, preferred_element_type=jnp.float32)
            )
        return jnp.concatenate(parts, axis=1)

    def visit_slab(partner, step_index, holder):
        owner = (chan_index - step_index) % chan_count
        block = lax.psum_scatter(
            slab_block(partner).astype(jnp.bfloat16), "tm", scatter_dimension=0, tiled=True
        ).astype(jnp.float32)
        return lax.dynamic_update_slice_in_dim(holder, block, owner * width, 2)

    def advance_slab(step_index, carry):
        partner, holder = carry
        partner = shifted(partner, "chan", 1)
        return (partner, visit_slab(partner, step_index, holder))

    collected = visit_slab(framed, 0, collected)
    moved_last, collected = lax.fori_loop(1, chan_count, advance_slab, (framed, collected))
    scaled = collected * (1.0 / math.sqrt(segs * length))
    return jnp.where(keep, scaled, 0.0).astype(jnp.bfloat16)


def solution(mesh):
    return jax.shard_map(
        on_device,
        mesh=mesh,
        in_specs=(P(None, "chan", "tm"), P(("chan", "tm")), P(), P(("chan", "tm"))),
        out_specs=P(("chan", "tm"), None, None),
        check_vma=False,
    )
```

profile of v0, /device:TPU:2, one launch (start us, length us, event | category | flops | bytes accessed | tf_op | source)
XLA Modules:
  0.0 1887.9 jit_solution(16198038434818797384)
XLA Ops:
  8.1 7.5 all-to-all-start
  26.5 157.4 %gather_fusion = f32[16384]{0:T(1024)S(1)} fusion(f32[2,2,4225]{2,1,0:T(2,128)S(1)} %concatenate.27, s32[16384]{0:T(1024)S(1)} %bitcast.1047), kind=kCustom, calls=%fused_computation.clone | custom fusion | bytes 327680 | tf_op jit(solution)/shard_map/jit(take_along_axis)/gather | solution.py:35
  183.9 157.4 %gather_fusion.1 = f32[16384]{0:T(1024)S(1)} fusion(f32[2,2,4225]{2,1,0:T(2,128)S(1)} %concatenate.27, s32[16384]{0:T(1024)S(1)} %bitcast.1046), kind=kCustom, calls=%fused_computation.1.clone | custom fusion | bytes 327680 | tf_op jit(solution)/shard_map/jit(take_along_axis)/gather | solution.py:35
  350.7 13.4 all_to_all.33
  385.4 7.6 stack.1771
  408.4 8.0 stack.1815
  434.1 8.4 stack.1859
  445.2 72.3 %reduce-scatter.3.cloned.1.call-done = bf16[2,129,32]{1,2,0:T(8,128)(2,1)} async-done(((bf16[32,129,32]{1,2,0:T(8,128)(2,1)}), bf16[2,129,32]{1,2,0:T(8,128)(2,1)}) %reduce-scatter.3.cloned.1.call-update) | async-done | bytes 16528 | tf_op jit(solution)/shard_map/reduce_scatter | solution.py:176
  518.5 6.7 dynamic_update_slice.13
  526.6 1351.8 %while.17 = (s32[]{:T(128)}, bf16[2,32,384]{2,1,0:T(8,128)(2,1)S(1)}, f32[2,129,512]{1,2,0:T(8,128)}, bf16[2,32,256]{2,1,0:T(8,128)(2,1)S(1)}, s32[]{:T(128)}, /...) while((s32[]{:T(128)}, bf16[2,32,384]{2,1,0:T(8,128)(2,1)S(1)}, ...), condition=%wide.region_7.9_spmd, body=%wide.region_5.8_spmd.sunk | while | flops 136199248 | bytes 15612520 | solution.py:187
  526.6 17.3 collective-permute-start
  557.7 71.2 %reduce-scatter.5.cloned.1.call-done = bf16[2,129,32]{1,2,0:T(8,128)(2,1)} async-done(((bf16[32,129,32]{1,2,0:T(8,128)(2,1)}), bf16[2,129,32]{1,2,0:T(8,128)(2,1)}) %reduce-scatter.5.cloned.1.call-update) | async-done | bytes 16528 | tf_op jit(solution)/shard_map/while/body/eval_jaxpr/reduce_scatter | solution.py:176
  645.9 72.3 %reduce-scatter.5.cloned.1.call-done = bf16[2,129,32]{1,2,0:T(8,128)(2,1)} async-done(((bf16[32,129,32]{1,2,0:T(8,128)(2,1)}), bf16[2,129,32]{1,2,0:T(8,128)(2,1)}) %reduce-scatter.5.cloned.1.call-update) | async-done | bytes 16528 | tf_op jit(solution)/shard_map/while/body/eval_jaxpr/reduce_scatter | solution.py:176
  720.1 5.6 collective-permute-done
  735.1 72.2 %reduce-scatter.5.cloned.1.call-done = bf16[2,129,32]{1,2,0:T(8,128)(2,1)} async-done(((bf16[32,129,32]{1,2,0:T(8,128)(2,1)}), bf16[2,129,32]{1,2,0:T(8,128)(2,1)}) %reduce-scatter.5.cloned.1.call-update) | async-done | bytes 16528 | tf_op jit(solution)/shard_map/while/body/eval_jaxpr/reduce_scatter | solution.py:176
  809.2 5.6 collective-permute-done
  824.2 72.2 %reduce-scatter.5.cloned.1.call-done = bf16[2,129,32]{1,2,0:T(8,128)(2,1)} async-done(((bf16[32,129,32]{1,2,0:T(8,128)(2,1)}), bf16[2,129,32]{1,2,0:T(8,128)(2,1)}) %reduce-scatter.5.cloned.1.call-update) | async-done | bytes 16528 | tf_op jit(solution)/shard_map/while/body/eval_jaxpr/reduce_scatter | solution.py:176
  898.4 5.6 collective-permute-done
  913.3 72.3 %reduce-scatter.5.cloned.1.call-done = bf16[2,129,32]{1,2,0:T(8,128)(2,1)} async-done(((bf16[32,129,32]{1,2,0:T(8,128)(2,1)}), bf16[2,129,32]{1,2,0:T(8,128)(2,1)}) %reduce-scatter.5.cloned.1.call-update) | async-done | bytes 16528 | tf_op jit(solution)/shard_map/while/body/eval_jaxpr/reduce_scatter | solution.py:176
  1002.5 72.3 %reduce-scatter.5.cloned.1.call-done = bf16[2,129,32]{1,2,0:T(8,128)(2,1)} async-done(((bf16[32,129,32]{1,2,0:T(8,128)(2,1)}), bf16[2,129,32]{1,2,0:T(8,128)(2,1)}) %reduce-scatter.5.cloned.1.call-update) | async-done | bytes 16528 | tf_op jit(solution)/shard_map/while/body/eval_jaxpr/reduce_scatter | solution.py:176
  1076.8 5.6 collective-permute-done
  1091.7 72.2 %reduce-scatter.5.cloned.1.call-done = bf16[2,129,32]{1,2,0:T(8,128)(2,1)} async-done(((bf16[32,129,32]{1,2,0:T(8,128)(2,1)}), bf16[2,129,32]{1,2,0:T(8,128)(2,1)}) %reduce-scatter.5.cloned.1.call-update) | async-done | bytes 16528 | tf_op jit(solution)/shard_map/while/body/eval_jaxpr/reduce_scatter | solution.py:176
  1180.8 72.2 %reduce-scatter.5.cloned.1.call-done = bf16[2,129,32]{1,2,0:T(8,128)(2,1)} async-done(((bf16[32,129,32]{1,2,0:T(8,128)(2,1)}), bf16[2,129,32]{1,2,0:T(8,128)(2,1)}) %reduce-scatter.5.cloned.1.call-update) | async-done | bytes 16528 | tf_op jit(solution)/shard_map/while/body/eval_jaxpr/reduce_scatter | solution.py:176
  1269.9 72.3 %reduce-scatter.5.cloned.1.call-done = bf16[2,129,32]{1,2,0:T(8,128)(2,1)} async-done(((bf16[32,129,32]{1,2,0:T(8,128)(2,1)}), bf16[2,129,32]{1,2,0:T(8,128)(2,1)}) %reduce-scatter.5.cloned.1.call-update) | async-done | bytes 16528 | tf_op jit(solution)/shard_map/while/body/eval_jaxpr/reduce_scatter | solution.py:176
  1344.1 5.6 collective-permute-done
  1359.1 72.3 %reduce-scatter.5.cloned.1.call-done = bf16[2,129,32]{1,2,0:T(8,128)(2,1)} async-done(((bf16[32,129,32]{1,2,0:T(8,128)(2,1)}), bf16[2,129,32]{1,2,0:T(8,128)(2,1)}) %reduce-scatter.5.cloned.1.call-update) | async-done | bytes 16528 | tf_op jit(solution)/shard_map/while/body/eval_jaxpr/reduce_scatter | solution.py:176
  1448.2 72.2 %reduce-scatter.5.cloned.1.call-done = bf16[2,129,32]{1,2,0:T(8,128)(2,1)} async-done(((bf16[32,129,32]{1,2,0:T(8,128)(2,1)}), bf16[2,129,32]{1,2,0:T(8,128)(2,1)}) %reduce-scatter.5.cloned.1.call-update) | async-done | bytes 16528 | tf_op jit(solution)/shard_map/while/body/eval_jaxpr/reduce_scatter | solution.py:176
  1537.4 72.2 %reduce-scatter.5.cloned.1.call-done = bf16[2,129,32]{1,2,0:T(8,128)(2,1)} async-done(((bf16[32,129,32]{1,2,0:T(8,128)(2,1)}), bf16[2,129,32]{1,2,0:T(8,128)(2,1)}) %reduce-scatter.5.cloned.1.call-update) | async-done | bytes 16528 | tf_op jit(solution)/shard_map/while/body/eval_jaxpr/reduce_scatter | solution.py:176
  1626.5 72.2 %reduce-scatter.5.cloned.1.call-done = bf16[2,129,32]{1,2,0:T(8,128)(2,1)} async-done(((bf16[32,129,32]{1,2,0:T(8,128)(2,1)}), bf16[2,129,32]{1,2,0:T(8,128)(2,1)}) %reduce-scatter.5.cloned.1.call-update) | async-done | bytes 16528 | tf_op jit(solution)/shard_map/while/body/eval_jaxpr/reduce_scatter | solution.py:176
  1700.6 5.6 collective-permute-done
  1715.6 72.2 %reduce-scatter.5.cloned.1.call-done = bf16[2,129,32]{1,2,0:T(8,128)(2,1)} async-done(((bf16[32,129,32]{1,2,0:T(8,128)(2,1)}), bf16[2,129,32]{1,2,0:T(8,128)(2,1)}) %reduce-scatter.5.cloned.1.call-update) | async-done | bytes 16528 | tf_op jit(solution)/shard_map/while/body/eval_jaxpr/reduce_scatter | solution.py:176
  1804.7 72.3 %reduce-scatter.5.cloned.1.call-done = bf16[2,129,32]{1,2,0:T(8,128)(2,1)} async-done(((bf16[32,129,32]{1,2,0:T(8,128)(2,1)}), bf16[2,129,32]{1,2,0:T(8,128)(2,1)}) %reduce-scatter.5.cloned.1.call-update) | async-done | bytes 16528 | tf_op jit(solution)/shard_map/while/body/eval_jaxpr/reduce_scatter | solution.py:176
  (1243 shorter events, 290.1 us)
Async XLA Ops:
  8.1 15.7 all-to-all-start
  15.5 501.9 %reduce-scatter.3.cloned.1.call-start = ((), (), s32[]{:S(2)}) async-start(), calls=%async_computation.4 | async-start | bytes 557056 | tf_op jit(solution)/shard_map/reduce_scatter | solution.py:176
  526.6 102.4 %reduce-scatter.5.cloned.1.call-start = ((), (), s32[]{:S(2)}) async-start(), calls=%async_computation.5 | async-start | bytes 557056 | tf_op jit(solution)/shard_map/while/body/eval_jaxpr/reduce_scatter | solution.py:176
  526.6 21.9 %collective-permute-start = (bf16[2,32,384]{2,1,0:T(8,128)(2,1)S(1)}, bf16[2,32,384]{2,1,0:T(8,128)(2,1)S(1)}, u32[]{:S(2)}, u32[]{:S(2)}) collective-permute-start(bf16[2,32,384]{2,1,0:T(8,128)(2,1)S(1)} %get-tuple-element.893), channel_id=1, source_target_pairs={{0,16},{16,32},{32,48},{48,64},{64,80},{80,96},{96,112},{112,128},... | collective-permute-start | bytes 147464 | tf_op jit(solution)/shard_map/while/body/eval_jaxpr/ppermute | solution.py:19
  630.3 87.8 %reduce-scatter.5.cloned.1.call-start = ((), (), s32[]{:S(2)}) async-start(), calls=%async_computation.5 | async-start | bytes 557056 | tf_op jit(solution)/shard_map/while/body/eval_jaxpr/reduce_scatter | solution.py:176
  630.3 6.2 collective-permute-start
  719.5 87.7 %reduce-scatter.5.cloned.1.call-start = ((), (), s32[]{:S(2)}) async-start(), calls=%async_computation.5 | async-start | bytes 557056 | tf_op jit(solution)/shard_map/while/body/eval_jaxpr/reduce_scatter | solution.py:176
  719.5 6.2 collective-permute-start
  808.7 87.8 %reduce-scatter.5.cloned.1.call-start = ((), (), s32[]{:S(2)}) async-start(), calls=%async_computation.5 | async-start | bytes 557056 | tf_op jit(solution)/shard_map/while/body/eval_jaxpr/reduce_scatter | solution.py:176
  808.7 6.2 collective-permute-start
  897.8 87.8 %reduce-scatter.5.cloned.1.call-start = ((), (), s32[]{:S(2)}) async-start(), calls=%async_computation.5 | async-start | bytes 557056 | tf_op jit(solution)/shard_map/while/body/eval_jaxpr/reduce_scatter | solution.py:176
  897.8 6.2 collective-permute-start
  986.9 87.9 %reduce-scatter.5.cloned.1.call-start = ((), (), s32[]{:S(2)}) async-start(), calls=%async_computation.5 | async-start | bytes 557056 | tf_op jit(solution)/shard_map/while/body/eval_jaxpr/reduce_scatter | solution.py:176
  986.9 6.2 collective-permute-start
  1076.2 87.7 %reduce-scatter.5.cloned.1.call-start = ((), (), s32[]{:S(2)}) async-start(), calls=%async_computation.5 | async-start | bytes 557056 | tf_op jit(solution)/shard_map/while/body/eval_jaxpr/reduce_scatter | solution.py:176
  1076.2 6.2 collective-permute-start
  1165.3 87.7 %reduce-scatter.5.cloned.1.call-start = ((), (), s32[]{:S(2)}) async-start(), calls=%async_computation.5 | async-start | bytes 557056 | tf_op jit(solution)/shard_map/while/body/eval_jaxpr/reduce_scatter | solution.py:176
  1165.3 6.2 collective-permute-start
  1254.4 87.8 %reduce-scatter.5.cloned.1.call-start = ((), (), s32[]{:S(2)}) async-start(), calls=%async_computation.5 | async-start | bytes 557056 | tf_op jit(solution)/shard_map/while/body/eval_jaxpr/reduce_scatter | solution.py:176
  1254.4 6.2 collective-permute-start
  1343.6 87.8 %reduce-scatter.5.cloned.1.call-start = ((), (), s32[]{:S(2)}) async-start(), calls=%async_computation.5 | async-start | bytes 557056 | tf_op jit(solution)/shard_map/while/body/eval_jaxpr/reduce_scatter | solution.py:176
  1343.6 6.2 collective-permute-start
  1432.7 87.7 %reduce-scatter.5.cloned.1.call-start = ((), (), s32[]{:S(2)}) async-start(), calls=%async_computation.5 | async-start | bytes 557056 | tf_op jit(solution)/shard_map/while/body/eval_jaxpr/reduce_scatter | solution.py:176
  1432.7 6.2 collective-permute-start
  1521.8 87.7 %reduce-scatter.5.cloned.1.call-start = ((), (), s32[]{:S(2)}) async-start(), calls=%async_computation.5 | async-start | bytes 557056 | tf_op jit(solution)/shard_map/while/body/eval_jaxpr/reduce_scatter | solution.py:176
  1521.8 6.2 collective-permute-start
  1611.0 87.7 %reduce-scatter.5.cloned.1.call-start = ((), (), s32[]{:S(2)}) async-start(), calls=%async_computation.5 | async-start | bytes 557056 | tf_op jit(solution)/shard_map/while/body/eval_jaxpr/reduce_scatter | solution.py:176
  1611.0 6.2 collective-permute-start
  1700.1 87.7 %reduce-scatter.5.cloned.1.call-start = ((), (), s32[]{:S(2)}) async-start(), calls=%async_computation.5 | async-start | bytes 557056 | tf_op jit(solution)/shard_map/while/body/eval_jaxpr/reduce_scatter | solution.py:176
  1700.1 6.2 collective-permute-start
  1789.1 87.8 %reduce-scatter.5.cloned.1.call-start = ((), (), s32[]{:S(2)}) async-start(), calls=%async_computation.5 | async-start | bytes 557056 | tf_op jit(solution)/shard_map/while/body/eval_jaxpr/reduce_scatter | solution.py:176
  1789.1 6.2 collective-permute-start
  (86 other events, 399.8 us)
Sparse Core Ops, SparseCore 0:
  445.2 72.2 reduce-scatter.2
  557.8 71.0 reduce-scatter.4
  645.9 72.1 reduce-scatter.4
  735.1 72.1 reduce-scatter.4
  824.3 72.1 reduce-scatter.4
  913.4 72.1 reduce-scatter.4
  1002.5 72.2 reduce-scatter.4
  1091.8 72.0 reduce-scatter.4
  1180.9 72.0 reduce-scatter.4
  1270.0 72.1 reduce-scatter.4
  1359.2 72.1 reduce-scatter.4
  1448.3 72.1 reduce-scatter.4
  1537.4 72.0 reduce-scatter.4
  1626.5 72.0 reduce-scatter.4
  1715.7 72.0 reduce-scatter.4
  1804.7 72.1 reduce-scatter.4
where the time goes:
time: 1900 us; the launch traced here: 1890 us
  waiting for transfers between devices  1240 us (65%)
  local copies, waits for them, and re-layouts  499 us (26%)
  other arithmetic  47.3 us (2%)
  starting transfers between devices  33.1 us (2%)
  matrix products  31.1 us (2%)
  between operations  19.4 us (1%)
    reduce_scatter x16, waiting for transfers between devices, visit_slab(): lax.psum_scatter(slab_block(partner).astype(jnp.bfloat16), 'tm', scatter_...  1150 us
    gather x2, local copies, waits for them, and re-layouts, window_mean(): jnp.take_along_axis(running, upper_index, axis=2)  157 us
    gather x2, local copies, waits for them, and re-layouts, window_mean(): jnp.take_along_axis(running, lower_index, axis=2)  157 us
    ppermute x15, waiting for transfers between devices, shifted(): lax.ppermute(value, axis, [(i, (i + by) % length) for i in range(length)])  83.1 us
    another operation x170, local copies, waits for them, and re-layouts, slab_block(): jnp.stack([partner[:, :, offset:offset + span] for offset in range(block_...  75.1 us
    while x645, local copies, waits for them, and re-layouts  60.9 us
  transfers between devices with their start and end apart: 32, of which 31 were waited for; matrix products, arithmetic and copies ran while one was open for 0% of the time, Pallas kernels for 0%

commit v1 on v0

v1 whole, which is shorter than its diff:
```python
import functools
import math

import jax
import jax.numpy as jnp
import ml_dtypes
import numpy as np
from jax import lax
from jax.experimental import pallas as pl
from jax.experimental.pallas import tpu as pltpu
from jax.sharding import PartitionSpec as P

LAG = 64
TINY = 1e-05
NT = 4096
Q = 32
GROUPS = 4
LINE = 2 * (NT + LAG)
STEP = 16
A_BLOCKS = 2 * LAG // STEP
CHUNK = 13 * 128
BAND_LO = 16
BAND_HI = 1638
BINS = 64

bf16 = jnp.bfloat16
f32 = jnp.float32


def split_const(table):
    high = table.astype(ml_dtypes.bfloat16)
    low = (table - high.astype(np.float64)).astype(ml_dtypes.bfloat16)
    return high, low


@functools.lru_cache(maxsize=None)
def tables():
    q = np.arange(Q)
    p = np.arange(128)
    eye = np.eye(GROUPS)
    ang_q = 2 * np.pi * np.outer(q, q) / Q
    cos_q, sin_q = np.kron(eye, np.cos(ang_q)), np.kron(eye, np.sin(ang_q))
    first = np.concatenate([cos_q, -sin_q], axis=0)
    last = np.concatenate([cos_q, -sin_q], axis=1)
    ang_t = 2 * np.pi * np.outer(q, p) / NT
    twiddle = np.concatenate([np.tile(np.cos(ang_t), (GROUPS, 1)), np.tile(np.sin(ang_t), (GROUPS, 1))], axis=0)
    ang_p = 2 * np.pi * np.outer(p, np.arange(BINS) - 1) / 128
    cos_p, sin_p = np.cos(ang_p), np.sin(ang_p)
    second = np.block([[cos_p, -sin_p], [sin_p, cos_p]])
    third = np.block([[cos_p.T, sin_p.T], [-sin_p.T, cos_p.T]])
    tri = np.concatenate([
        np.kron(eye, np.ones((Q, Q))),
        np.kron(eye, (q[None, :] >= q[:, None]).astype(float)),
        np.kron(eye, (q[None, :] <= q[:, None]).astype(float)),
    ], axis=0)
    out = []
    for table in (first, second, third, last):
        out.extend(split_const(table))
    out.append(tri.astype(ml_dtypes.bfloat16))
    out.append(twiddle.astype(np.float32))
    return out


def parts2(x):
    high = x.astype(bf16)
    return high, (x - high.astype(f32)).astype(bf16)


def parts3(x):
    high = x.astype(bf16)
    rest = x - high.astype(f32)
    mid = rest.astype(bf16)
    return high, mid, (rest - mid.astype(f32)).astype(bf16)


def dot(a, b):
    return jnp.dot(a, b, preferred_element_type=f32)


def right_product(x, high, low):
    xh, xl = parts2(x)
    return dot(xh, high) + (dot(xl, high) + dot(xh, low))


def left_product(high, low, x):
    xh, xl = parts2(x)
    return dot(high, xh) + (dot(high, xl) + dot(low, xh))


def whiten_kernel(alive, starts, halves, x_ref, first_h, first_l, second_h, second_l, third_h, third_l,
                  last_h, last_l, tri_ref, twid_ref, out_ref, sig, pad):
    lane = lax.broadcasted_iota(jnp.int32, (Q, 128), 1)
    sig[...] = jnp.zeros_like(sig)
    pad[...] = jnp.zeros_like(pad)
    normed = []
    for r in range(2):
        gate = alive[r].astype(f32)
        half = halves[r]
        for s in range(2):
            base = (r * 2 + s) * 48
            for h in range(2):
                piece = x_ref[pl.ds(s * 4 + r * 2 + h, 16, stride=8), :]
                sig[pl.ds(base + h, 16, stride=2), :] = piece * gate
            start = starts[s]
            whole = start // 128
            part = start % 128
            here = sig[pl.ds(base + whole, Q), :]
            after = sig[pl.ds(base + whole + 1, Q), :]
            turn = lax.rem(128 - part, 128)
            moved = jnp.where(lane + part < 128, pltpu.roll(here, turn, 1), pltpu.roll(after, turn, 1))
            pad[pl.ds(base + 8, Q), :] = moved
        row = lax.broadcasted_iota(jnp.int32, (128, 128), 0)
        col = lax.broadcasted_iota(jnp.int32, (128, 128), 1)
        gap = row - col
        bands = (gap >= 128 - half, jnp.abs(gap) <= half, -gap >= 128 - half)
        total = None
        signal = jnp.concatenate([pad[pl.ds((r * 2 + s) * 48 + 8, Q), :] for s in range(2)], axis=0)
        for k, band in enumerate(bands):
            weight = jnp.where(band, 1.0, 0.0).astype(bf16)
            value = jnp.concatenate([pad[pl.ds((r * 2 + s) * 48 + 7 + k, Q), :] for s in range(2)], axis=0)
            for term in parts3(jnp.abs(value)):
                add = dot(term, weight)
                total = add if total is None else total + add
        level = total / (2 * half + 1).astype(f32)
        normed.append(signal / (level + TINY))
    x = jnp.concatenate(normed, axis=0)
    cos_t = twid_ref[0:128, :]
    sin_t = twid_ref[128:256, :]
    stage = left_product(first_h[...], first_l[...], x)
    re, im = stage[0:128], stage[128:256]
    turned = jnp.concatenate([re * cos_t + im * sin_t, im * cos_t - re * sin_t], axis=1)
    spec = right_product(turned, second_h[...], second_l[...])
    square = spec * spec
    size = jnp.sqrt(square + pltpu.roll(square, BINS, 1))
    sums = None
    for term in parts3(size):
        add = dot(tri_ref[...], term)
        sums = add if sums is None else sums + add
    smooth = (sums[0:128] + pltpu.roll(sums[128:256], 1, 1) + pltpu.roll(sums[256:384], 127, 1)) / 65.0
    k1 = lax.broadcasted_iota(jnp.int32, (128, 128), 0) % Q
    jj = lax.broadcasted_iota(jnp.int32, (128, 128), 1) % BINS
    bins = k1 + Q * (jj - 1)
    band = (bins >= BAND_LO) & (bins <= BAND_HI)
    gain = jnp.where(band, 2.0 / math.sqrt(NT), 0.0) / (smooth + TINY)
    stage = right_product(spec * gain, third_h[...], third_l[...])
    re, im = stage[:, 0:128], stage[:, 128:256]
    turned = jnp.concatenate([re * cos_t - im * sin_t, im * cos_t + re * sin_t], axis=0)
    white = left_product(last_h[...], last_l[...], turned)
    rolled = pltpu.roll(white, 64, 1)
    for r in range(2):
        sig[pl.ds(r * 40, Q), :] = white[r * 64:r * 64 + Q]
        pad[pl.ds(r * 48 + 8, Q), :] = rolled[r * 64 + Q:r * 64 + 2 * Q]
        pad[pl.ds(r * 48 + 40, 8), :] = jnp.zeros((8, 128), f32)
        pad[pl.ds(r * 48, 8), :] = jnp.zeros((8, 128), f32)
    low = lax.broadcasted_iota(jnp.int32, (2, 128), 1) < 64
    for m in range(Q):
        out_ref[:, m * 128:(m + 1) * 128] = sig[pl.ds(m, 2, stride=40), :].astype(bf16)
    for m in range(Q + 1):
        a = pad[pl.ds(7 + m, 2, stride=48), :]
        b = pad[pl.ds(8 + m, 2, stride=48), :]
        out_ref[:, (Q + m) * 128:(Q + m + 1) * 128] = jnp.where(low, a, b).astype(bf16)


def whiten(x, alive, starts, halves):
    consts = [jnp.asarray(t) for t in tables()]
    smem = pl.BlockSpec(memory_space=pltpu.SMEM)
    vmem = pl.BlockSpec(memory_space=pltpu.VMEM)
    return pl.pallas_call(
        whiten_kernel,
        out_shape=jax.ShapeDtypeStruct((2, LINE), bf16),
        in_specs=[smem] * 3 + [vmem] * (1 + len(consts)),
        out_specs=vmem,
        scratch_shapes=[pltpu.VMEM((4 * 48, 128), f32), pltpu.VMEM((4 * 48, 128), f32)],
        name="whiten",
    )(alive, starts, halves, x, *consts)


def corr_kernel(xi_ref, xj_ref, out_ref, xi, xj, acc, left, right, tall, form):
    for src, dst in ((xi_ref, xi), (xj_ref, xj)):
        dst[:, 128:128 + LINE] = src[...]
        dst[:, 0:128] = src[:, LINE - 128:LINE]
        dst[:, 128 + LINE:256 + LINE] = src[:, 0:128]
    acc[...] = jnp.zeros_like(acc)

    @pl.loop(0, LINE // CHUNK)
    def _(step):
        at = pl.multiple_of(step * CHUNK, 128)
        wide = CHUNK + 256
        line_i = xi[:, pl.ds(at, wide)]
        line_j = xj[:, pl.ds(at, wide)]
        for a in range(A_BLOCKS + 1):
            shift = (STEP * a - LAG) % wide
            moved = pltpu.roll(line_i, shift, 1) if shift else line_i
            left[a * 32:(a + 1) * 32, :] = moved[:, 128:128 + CHUNK]
        for b in range(STEP):
            moved = pltpu.roll(line_j, wide - b, 1) if b else line_j
            right[b * 32:(b + 1) * 32, :] = moved[:, 128:128 + CHUNK]
        acc[...] += lax.dot_general(left[...], right[...], (((1,), (1,)), ((), ())), preferred_element_type=f32)

    scale = 1.0 / math.sqrt(2 * NT)
    for bh in range(4):
        tall[bh * 288:(bh + 1) * 288, :] = acc[:, bh * 128:(bh + 1) * 128] * scale
    form[64:72, :] = jnp.zeros((8, 128), f32)
    for t in range(16):
        for bh in range(4):
            for r in range(2):
                form[bh * 16 + r * 8:bh * 16 + r * 8 + 8, :] = tall[pl.ds(bh * 288 + t * 2 + r, 8, stride=32), :]
        form[64:66, :] = tall[256 + t * 2:258 + t * 2, :]
        out_ref[t] = form[...].astype(bf16)


def correlate(xi, xj):
    vmem = pl.BlockSpec(memory_space=pltpu.VMEM)
    rows = 32 * (A_BLOCKS + 1)
    cols = 32 * STEP
    return pl.pallas_call(
        corr_kernel,
        out_shape=jax.ShapeDtypeStruct((16, 72, 128), bf16),
        in_specs=[vmem] * 2,
        out_specs=vmem,
        scratch_shapes=[
            pltpu.VMEM((32, LINE + 256), bf16), pltpu.VMEM((32, LINE + 256), bf16),
            pltpu.VMEM((rows, cols), f32), pltpu.VMEM((rows, CHUNK), bf16), pltpu.VMEM((cols, CHUNK), bf16),
            pltpu.VMEM((4 * rows, 128), f32), pltpu.VMEM((72, 128), f32),
        ],
        compiler_params=pltpu.CompilerParams(vmem_limit_bytes=48 << 20),
        name="correlate",
    )(xi, xj)


def place_kernel(own, x_ref, perm_ref, out_ref, rows, res):
    lane = lax.broadcasted_iota(jnp.int32, (16, 128), 1) // 32

    def turn(value, by):
        by = by % 128
        return pltpu.roll(value, by, 1) if by else value

    for hi in range(4):
        for bh in range(5):
            source = [x_ref[hi * 4 + lo, bh * 16:bh * 16 + 16, :].astype(f32) if bh < 4 else
                      jnp.concatenate([x_ref[hi * 4 + lo, 64:72, :].astype(f32)] * 2, axis=0) for lo in range(4)]
            for bl in range(4 if bh < 4 else 1):
                value = turn(source[0], -32 * bl)
                for lo in range(1, 4):
                    value = jnp.where(lane == lo, turn(source[lo], 32 * (lo - bl)), value)
                at = (bh * 4 + bl) * 16
                rows[at:at + 16, hi * 128:(hi + 1) * 128] = value.astype(bf16)
    moved = dot(rows[...], perm_ref[...])
    row = lax.broadcasted_iota(jnp.int32, moved.shape, 0)
    col = lax.broadcasted_iota(jnp.int32, moved.shape, 1)
    which = jnp.where(row < 256, (row // 8) % 2, row % 2)
    moved = jnp.where(col == own[0] + which, 0.0, moved)
    for hi in range(4):
        span = slice(hi * 128, (hi + 1) * 128)
        res[hi * 272:(hi + 1) * 272, :] = moved[:, span]
        for b in range(16):
            for a in range(8):
                out_ref[16 * a + b, :, span] = res[pl.ds(hi * 272 + b * 16 + a, 2, stride=8), :].astype(bf16)
        out_ref[128, :, span] = res[hi * 272 + 256:hi * 272 + 258, :].astype(bf16)


def place(own, x, perm):
    smem = pl.BlockSpec(memory_space=pltpu.SMEM)
    vmem = pl.BlockSpec(memory_space=pltpu.VMEM)
    return pl.pallas_call(
        place_kernel,
        out_shape=jax.ShapeDtypeStruct((129, 2, 512), bf16),
        in_specs=[smem, vmem, vmem],
        out_specs=vmem,
        scratch_shapes=[pltpu.VMEM((272, 512), bf16), pltpu.VMEM((4 * 272, 128), f32)],
        name="place",
    )(own, x, perm)


def on_device(raw, alive, seg_start, norm_half):
    chan_index = lax.axis_index("chan")
    time_index = lax.axis_index("tm")
    sent = raw.reshape(2, 16, 2, 2, 128).transpose(1, 0, 2, 3, 4).reshape(16, 8, 128)
    traces = lax.all_to_all(sent, "tm", split_axis=0, concat_axis=0, tiled=True).reshape(128, 128)
    white = whiten(traces, alive, seg_start, norm_half)
    spread = jnp.broadcast_to(white[None], (16, 2, LINE))
    rows = lax.all_to_all(spread, "tm", split_axis=0, concat_axis=0, tiled=True).reshape(32, LINE)
    cols = lax.all_gather(white, "chan", axis=0, tiled=True)
    block = correlate(rows, cols)
    back = lax.all_to_all(block, "tm", split_axis=0, concat_axis=0, tiled=True)
    lanes = jnp.arange(512, dtype=jnp.int32)
    holder = lanes // 32
    group = (lanes % 32) // 2
    target = group * 32 + holder * 2 + lanes % 2
    perm = (target[:, None] == lanes[None, :]).astype(bf16)
    own = ((chan_index * 16 + time_index) * 2).astype(jnp.int32).reshape(1)
    return place(own, back, perm).transpose(1, 0, 2)


def solution(mesh):
    return jax.shard_map(
        on_device,
        mesh=mesh,
        in_specs=(P(None, "chan", "tm"), P(("chan", "tm")), P(), P(("chan", "tm"))),
        out_specs=P(("chan", "tm"), None, None),
        check_vma=False,
    )
```

time: 1900 us -> 94.8 us (0.05)
  the two profiles are of different devices: /device:TPU:2 before, /device:TPU:1 now
where the time goes in v1:
time: 94.8 us; the launch traced here: 94.3 us
  blocking collectives  48.5 us (51%)
  starting transfers between devices  20.6 us (22%)
  Pallas kernels  12.1 us (13%)
  waiting for transfers between devices  8.26 us (9%)
  local copies, waits for them, and re-layouts  3.82 us (4%)
  other arithmetic  0.95 us (1%)
    all_gather x1, blocking collectives, on_device(): cols = lax.all_gather(white, 'chan', axis=0, tiled=True)  32.8 us
    all_to_all x1, starting transfers between devices, on_device(): back = lax.all_to_all(block, 'tm', split_axis=0, concat_axis=0, tiled=True)  16.7 us
    all_to_all x1, blocking collectives, on_device(): lax.all_to_all(sent, 'tm', split_axis=0, concat_axis=0, tiled=True)  15.7 us
    all_to_all x1, waiting for transfers between devices, on_device(): back = lax.all_to_all(block, 'tm', split_axis=0, concat_axis=0, tiled=True)  8.25 us
    pallas_call x1, Pallas kernels, correlate(): pl.pallas_call(corr_kernel, out_shape=jax.ShapeDtypeStruct((16, 72, 128),...  6.01 us
    all_to_all x1, starting transfers between devices, on_device(): lax.all_to_all(spread, 'tm', split_axis=0, concat_axis=0, tiled=True)  3.89 us
    pallas_call x1, Pallas kernels, whiten(): pl.pallas_call(whiten_kernel, out_shape=jax.ShapeDtypeStruct((2, LINE), b...  3.6 us
    pallas_call x1, Pallas kernels, place(): pl.pallas_call(place_kernel, out_shape=jax.ShapeDtypeStruct((129, 2, 512)...  2.5 us
  transfers between devices with their start and end apart: 2, of which 1 were waited for; matrix products, arithmetic and copies ran while one was open for 1% of the time, Pallas kernels for 0%

profile of v1, /device:TPU:1, one launch (start us, length us, event | category | flops | bytes accessed | tf_op | source)
XLA Modules:
  0.0 94.3 jit_solution(10051352574053546267)
XLA Ops:
  0.0 0.9 reshape.63
  0.9 15.7 %all_to_all.15 = f32[16,8,128]{2,1,0:T(8,128)} all-to-all(f32[16,8,128]{2,1,0:T(8,128)S(1)} %bitcast.7), channel_id=1, replica_groups=mesh['chan'=16,'tm'=16] {'tm'}, dimensions={0} | all-to-all | bytes 131072 | tf_op jit(solution)/shard_map/all_to_all | solution.py:279
  16.6 3.6 %whiten.1 = bf16[2,8320]{1,0:T(2,128)(2,1)} custom-call(s32[2]{0:T(128)} %alive.1, s32[2]{0:T(128)} %starts.1, s32[2]{0:T(128)} %halves.1, f32[128,128]{1,0:T(8,128)} %bitcast.9, bf16[256,128]{1,0:T(8,128)(2,1)} %constant.81.clone.first_h, bf16[256,128]{1,0:T(8,128)(2,1)} %constant.82.clone.first_l, bf16[256,128]{1,0:T(8,128)(2,1)} %constant.83.clone.second_h, ...), custom_call_target="tpu_custom_call" | custom-call | tf_op jit(solution)/shard_map/whiten/pallas_call | solution.py:168
  20.2 1.8 %broadcast_in_dim.2 = bf16[16,2,8320]{2,1,0:T(2,128)(2,1)} broadcast(bf16[2,8320]{1,0:T(2,128)(2,1)} %whiten.1), dimensions={1,2} | broadcast | bytes 565760 | tf_op jit(solution)/shard_map/broadcast_in_dim | solution.py:281
  22.0 0.0 copy-start.1
  22.0 3.9 %all-to-all-start.1 = ((bf16[16,2,8320]{2,1,0:T(2,128)(2,1)}), bf16[16,2,8320]{2,1,0:T(2,128)(2,1)S(1)}, u32[]{:S(2)}, u32[]{:S(2)}) async-start(bf16[16,2,8320]{2,1,0:T(2,128)(2,1)} %broadcast_in_dim.2), calls=%async_computation.1 | async-start | bytes 1064960 | tf_op jit(solution)/shard_map/all_to_all | solution.py:282
  25.9 0.0 copy-done.1
  25.9 32.8 %all-gather = bf16[16,2,8320]{2,1,0:T(2,128)(2,1)S(1)} all-gather(bf16[1,2,8320]{2,1,0:T(2,128)(2,1)S(1)} %bitcast.6), channel_id=1, replica_groups=mesh['chan'=16,'tm'=16] {'chan'}, dimensions={0}, use_global_device_ids=true | all-gather | bytes 565760 | tf_op jit(solution)/shard_map/all_gather | solution.py:283
  58.7 0.2 reshape.68.xj_ref
  58.9 0.0 all-to-all-done.1
  58.9 0.2 reshape.66.xi_ref
  59.2 6.0 %correlate.1 = bf16[16,72,128]{2,1,0:T(8,128)(2,1)} custom-call(bf16[32,8320]{1,0:T(8,128)(2,1)S(1)} %reshape.66.xi_ref, bf16[32,8320]{1,0:T(8,128)(2,1)S(1)} %reshape.68.xj_ref), custom_call_target="tpu_custom_call" | custom-call | tf_op jit(solution)/shard_map/correlate/pallas_call | solution.py:216
  65.2 16.7 %all-to-all-start.2 = ((bf16[16,72,128]{2,1,0:T(8,128)(2,1)}), bf16[16,72,128]{2,1,0:T(8,128)(2,1)S(1)}, u32[]{:S(2)}, u32[]{:S(2)}) async-start(bf16[16,72,128]{2,1,0:T(8,128)(2,1)} %correlate.1), calls=%async_computation.2 | async-start | bytes 589824 | tf_op jit(solution)/shard_map/all_to_all | solution.py:285
  81.9 0.9 fusion.perm_ref
  82.8 8.3 %all-to-all-done.2.x_ref = bf16[16,72,128]{2,1,0:T(8,128)(2,1)S(1)} async-done(((bf16[16,72,128]{2,1,0:T(8,128)(2,1)}), bf16[16,72,128]{2,1,0:T(8,128)(2,1)S(1)}, u32[]{:S(2)}, u32[]{:S(2)}) %all-to-all-start.2) | async-done | bytes 294944 | tf_op jit(solution)/shard_map/all_to_all | solution.py:285
  91.1 0.0 copy-start
  91.1 0.7 copy-done
  91.8 2.5 %place.1 = bf16[129,2,512]{2,1,0:T(2,128)(2,1)} custom-call(s32[1]{0:T(128)} %bitcast.own, bf16[16,72,128]{2,1,0:T(8,128)(2,1)} %copy-done, bf16[512,512]{1,0:T(8,128)(2,1)} %fusion.perm_ref), custom_call_target="tpu_custom_call" | custom-call | tf_op jit(solution)/shard_map/place/pallas_call | solution.py:265
  (2 shorter events, 0.0 us)
Async XLA Ops:
  22.0 3.9 %copy-start.1 = (bf16[2,8320]{1,0:T(2,128)(2,1)S(1)}, bf16[2,8320]{1,0:T(2,128)(2,1)}, u32[]{:S(2)}) copy-start(bf16[2,8320]{1,0:T(2,128)(2,1)} %whiten.1) | copy-start | bytes 99844
  22.0 36.9 %all-to-all-start.1 = ((bf16[16,2,8320]{2,1,0:T(2,128)(2,1)}), bf16[16,2,8320]{2,1,0:T(2,128)(2,1)S(1)}, u32[]{:S(2)}, u32[]{:S(2)}) async-start(bf16[16,2,8320]{2,1,0:T(2,128)(2,1)} %broadcast_in_dim.2), calls=%async_computation.1 | async-start | bytes 1064960 | tf_op jit(solution)/shard_map/all_to_all | solution.py:282
  65.2 25.9 %all-to-all-start.2 = ((bf16[16,72,128]{2,1,0:T(8,128)(2,1)}), bf16[16,72,128]{2,1,0:T(8,128)(2,1)S(1)}, u32[]{:S(2)}, u32[]{:S(2)}) async-start(bf16[16,72,128]{2,1,0:T(8,128)(2,1)} %correlate.1), calls=%async_computation.2 | async-start | bytes 589824 | tf_op jit(solution)/shard_map/all_to_all | solution.py:285
  91.1 0.7 copy-start

commit v2 on v1

--- a/solution.py
+++ b/solution.py
@@ -8,7 +8,7 @@
 from jax import lax
 from jax.experimental import pallas as pl
 from jax.experimental.pallas import tpu as pltpu
-from jax.sharding import PartitionSpec as P
+from jax.sharding import Mesh, PartitionSpec as P
 
 LAG = 64
 TINY = 1e-05
@@ -88,7 +88,7 @@
 
 
 def whiten_kernel(alive, starts, halves, x_ref, first_h, first_l, second_h, second_l, third_h, third_l,
-                  last_h, last_l, tri_ref, twid_ref, out_ref, sig, pad):
+                  last_h, last_l, tri_ref, twid_ref, out_ref, spread_ref, sig, pad):
     lane = lax.broadcasted_iota(jnp.int32, (Q, 128), 1)
     sig[...] = jnp.zeros_like(sig)
     pad[...] = jnp.zeros_like(pad)
@@ -153,12 +153,15 @@
         pad[pl.ds(r * 48 + 40, 8), :] = jnp.zeros((8, 128), f32)
         pad[pl.ds(r * 48, 8), :] = jnp.zeros((8, 128), f32)
     low = lax.broadcasted_iota(jnp.int32, (2, 128), 1) < 64
-    for m in range(Q):
-        out_ref[:, m * 128:(m + 1) * 128] = sig[pl.ds(m, 2, stride=40), :].astype(bf16)
-    for m in range(Q + 1):
-        a = pad[pl.ds(7 + m, 2, stride=48), :]
-        b = pad[pl.ds(8 + m, 2, stride=48), :]
-        out_ref[:, (Q + m) * 128:(Q + m + 1) * 128] = jnp.where(low, a, b).astype(bf16)
+    for m in range(2 * Q + 1):
+        if m < Q:
+            value = sig[pl.ds(m, 2, stride=40), :]
+        else:
+            value = jnp.where(low, pad[pl.ds(7 + m - Q, 2, stride=48), :], pad[pl.ds(8 + m - Q, 2, stride=48), :])
+        value = value.astype(bf16)
+        out_ref[:, m * 128:(m + 1) * 128] = value
+        for e in range(16):
+            spread_ref[e, :, m * 128:(m + 1) * 128] = value
 
 
 def whiten(x, alive, starts, halves):
@@ -167,19 +170,28 @@
     vmem = pl.BlockSpec(memory_space=pltpu.VMEM)
     return pl.pallas_call(
         whiten_kernel,
-        out_shape=jax.ShapeDtypeStruct((2, LINE), bf16),
+        out_shape=(jax.ShapeDtypeStruct((2, LINE), bf16), jax.ShapeDtypeStruct((16, 2, LINE), bf16)),
         in_specs=[smem] * 3 + [vmem] * (1 + len(consts)),
-        out_specs=vmem,
+        out_specs=(vmem, vmem),
         scratch_shapes=[pltpu.VMEM((4 * 48, 128), f32), pltpu.VMEM((4 * 48, 128), f32)],
         name="whiten",
     )(alive, starts, halves, x, *consts)
 
 
-def corr_kernel(xi_ref, xj_ref, out_ref, xi, xj, acc, left, right, tall, form):
-    for src, dst in ((xi_ref, xi), (xj_ref, xj)):
-        dst[:, 128:128 + LINE] = src[...]
-        dst[:, 0:128] = src[:, LINE - 128:LINE]
-        dst[:, 128 + LINE:256 + LINE] = src[:, 0:128]
+def load_lines(refs, line):
+    at = 0
+    for ref in refs:
+        for k in range(ref.shape[0]):
+            line[at:at + 2, 128:128 + LINE] = ref[k]
+            at += 2
+    line[:, 0:128] = line[:, LINE:LINE + 128]
+    line[:, 128 + LINE:256 + LINE] = line[:, 128:256]
+
+
+def corr_kernel(rows_ref, *rest):
+    cols, (out_ref, xi, xj, acc, left, right, tall, form) = rest[:-8], rest[-8:]
+    load_lines([rows_ref], xi)
+    load_lines(cols, xj)
     acc[...] = jnp.zeros_like(acc)
 
     @pl.loop(0, LINE // CHUNK)
@@ -209,23 +221,24 @@
         out_ref[t] = form[...].astype(bf16)
 
 
-def correlate(xi, xj):
+def correlate(rows_in, cols_in):
     vmem = pl.BlockSpec(memory_space=pltpu.VMEM)
     rows = 32 * (A_BLOCKS + 1)
     cols = 32 * STEP
     return pl.pallas_call(
         corr_kernel,
         out_shape=jax.ShapeDtypeStruct((16, 72, 128), bf16),
-        in_specs=[vmem] * 2,
+        in_specs=[vmem] * (1 + len(cols_in)),
         out_specs=vmem,
         scratch_shapes=[
             pltpu.VMEM((32, LINE + 256), bf16), pltpu.VMEM((32, LINE + 256), bf16),
             pltpu.VMEM((rows, cols), f32), pltpu.VMEM((rows, CHUNK), bf16), pltpu.VMEM((cols, CHUNK), bf16),
             pltpu.VMEM((4 * rows, 128), f32), pltpu.VMEM((72, 128), f32),
         ],
-        compiler_params=pltpu.CompilerParams(vmem_limit_bytes=48 << 20),
+        compiler_params=pltpu.CompilerParams(vmem_limit_bytes=32 << 20),
+        cost_estimate=pl.CostEstimate(flops=2 * rows * cols * LINE, bytes_accessed=4 << 20, transcendentals=0),
         name="correlate",
-    )(xi, xj)
+    )(rows_in, *cols_in)
 
 
 def place_kernel(own, x_ref, perm_ref, out_ref, rows, res):
@@ -268,35 +281,54 @@
         in_specs=[smem, vmem, vmem],
         out_specs=vmem,
         scratch_shapes=[pltpu.VMEM((272, 512), bf16), pltpu.VMEM((4 * 272, 128), f32)],
+        compiler_params=pltpu.CompilerParams(vmem_limit_bytes=16 << 20),
         name="place",
     )(own, x, perm)
 
 
+PLANE = ("yl", "x", "yh")
+SLABS = ("x", "yh", "core")
+
+
+def passed(value, axis, by):
+    length = lax.axis_size(axis)
+    return lax.ppermute(value, axis, [(i, (i + by) % length) for i in range(length)])
+
+
 def on_device(raw, alive, seg_start, norm_half):
-    chan_index = lax.axis_index("chan")
-    time_index = lax.axis_index("tm")
+    z, yl, x, yh, core = (lax.axis_index(axis) for axis in ("z", "yl", "x", "yh", "core"))
     sent = raw.reshape(2, 16, 2, 2, 128).transpose(1, 0, 2, 3, 4).reshape(16, 8, 128)
-    traces = lax.all_to_all(sent, "tm", split_axis=0, concat_axis=0, tiled=True).reshape(128, 128)
-    white = whiten(traces, alive, seg_start, norm_half)
-    spread = jnp.broadcast_to(white[None], (16, 2, LINE))
-    rows = lax.all_to_all(spread, "tm", split_axis=0, concat_axis=0, tiled=True).reshape(32, LINE)
-    cols = lax.all_gather(white, "chan", axis=0, tiled=True)
-    block = correlate(rows, cols)
-    back = lax.all_to_all(block, "tm", split_axis=0, concat_axis=0, tiled=True)
-    lanes = jnp.arange(512, dtype=jnp.int32)
-    holder = lanes // 32
-    group = (lanes % 32) // 2
-    target = group * 32 + holder * 2 + lanes % 2
-    perm = (target[:, None] == lanes[None, :]).astype(bf16)
-    own = ((chan_index * 16 + time_index) * 2).astype(jnp.int32).reshape(1)
+    traces = lax.all_to_all(sent, SLABS, split_axis=0, concat_axis=0, tiled=True).reshape(128, 128)
+    white, spread = whiten(traces, alive, seg_start, norm_half)
+    rows = lax.all_to_all(spread, PLANE, split_axis=0, concat_axis=0, tiled=True)
+    white = white[None]
+    up, down = passed(white, "z", 1), passed(white, "z", -1)
+    near = jnp.concatenate([white, up, down], axis=0)
+    far_up = passed(near, "z", 3)
+    far_down = passed(jnp.concatenate([white, up], axis=0), "z", -3)
+    near_other = passed(near, "core", 1)
+    far_other = passed(jnp.concatenate([far_up, far_down], axis=0), "core", 1)
+    block = correlate(rows, [near, far_up, far_down, near_other, far_other])
+    back = lax.all_to_all(block, PLANE, split_axis=0, concat_axis=0, tiled=True)
+    k = np.arange(512)
+    e, half, j = k // 32, (k // 16) % 2, k % 16
+    offset = np.repeat([0, 7, 1, 5, 4, 6, 3, 2], 2)[j]
+    fixed = (e // 8) * 32 + ((e // 2) % 4) * 8 + (e % 2) * 4 + j % 2
+    from_z = (z + jnp.asarray(offset, jnp.int32)) & 7
+    target = from_z * 64 + jnp.asarray(fixed, jnp.int32) + (core ^ jnp.asarray(half, jnp.int32)) * 2
+    k = lax.iota(jnp.int32, 512)
+    perm = (target[:, None] == k[None, :]).astype(bf16)
+    own = (((z * 2 + yl) * 16 + x * 4 + yh * 2 + core) * 2).astype(jnp.int32).reshape(1)
     return place(own, back, perm).transpose(1, 0, 2)
 
 
 def solution(mesh):
+    fine = Mesh(mesh.devices.reshape(8, 2, 4, 2, 2), ("z", "yl", "x", "yh", "core"))
+    both = ("z", "yl", "x", "yh", "core")
     return jax.shard_map(
         on_device,
-        mesh=mesh,
-        in_specs=(P(None, "chan", "tm"), P(("chan", "tm")), P(), P(("chan", "tm"))),
-        out_specs=P(("chan", "tm"), None, None),
+        mesh=fine,
+        in_specs=(P(None, ("z", "yl"), SLABS), P(both), P(), P(both)),
+        out_specs=P(both, None, None),
         check_vma=False,
     )

time: 94.8 us -> 70.6 us (0.74)
  the two profiles are of different devices: /device:TPU:1 before, /device:TPU:2 now
where the time goes in v2:
time: 70.6 us; the launch traced here: 70.1 us
  starting transfers between devices  21.5 us (30%)
  waiting for transfers between devices  20.7 us (29%)
  blocking collectives  13.6 us (19%)
  Pallas kernels  11.9 us (17%)
  other arithmetic  1.4 us (2%)
  local copies, waits for them, and re-layouts  0.9 us (1%)
    all_to_all x1, blocking collectives, on_device(): lax.all_to_all(sent, SLABS, split_axis=0, concat_axis=0, tiled=True)  13.6 us
    ppermute x6, starting transfers between devices, passed(): lax.ppermute(value, axis, [(i, (i + by) % length) for i in range(length)])  11.6 us
    all_to_all x1, waiting for transfers between devices, on_device(): back = lax.all_to_all(block, PLANE, split_axis=0, concat_axis=0, tiled=True)  7.38 us
    all_to_all x1, waiting for transfers between devices, on_device(): lax.all_to_all(spread, PLANE, split_axis=0, concat_axis=0, tiled=True)  6.97 us
    pallas_call x1, Pallas kernels, correlate(): pl.pallas_call(corr_kernel, out_shape=jax.ShapeDtypeStruct((16, 72, 128),...  6.51 us
    ppermute x6, waiting for transfers between devices, passed(): lax.ppermute(value, axis, [(i, (i + by) % length) for i in range(length)])  6.38 us
    all_to_all x1, starting transfers between devices, on_device(): back = lax.all_to_all(block, PLANE, split_axis=0, concat_axis=0, tiled=True)  4.97 us
    all_to_all x1, starting transfers between devices, on_device(): lax.all_to_all(spread, PLANE, split_axis=0, concat_axis=0, tiled=True)  4.87 us
  transfers between devices with their start and end apart: 8, of which 5 were waited for; matrix products, arithmetic and copies ran while one was open for 1% of the time, Pallas kernels for 0%

profile of v2, /device:TPU:2, one launch (start us, length us, event | category | flops | bytes accessed | tf_op | source)
XLA Modules:
  0.0 70.1 jit_solution(8379091009897032650)
XLA Ops:
  0.0 0.9 %reshape.14 = f32[2,16,2,2,128]{4,3,2,1,0:T(2,128)S(1)} reshape(f32[2,32,256]{2,1,0:T(8,128)} %param.17) | data formatting | bytes 131072 | tf_op jit(solution)/shard_map/reshape | solution.py:300
  0.9 13.6 %all_to_all.15 = f32[16,8,128]{2,1,0:T(8,128)} all-to-all(f32[16,8,128]{2,1,0:T(8,128)S(1)} %bitcast.6), channel_id=1, replica_groups=mesh['z'=8,'yl'=2,'x'=4,'yh'=2,'core'=2] {'x','yh','core'}, dimensions={0} | all-to-all | bytes 131072 | tf_op jit(solution)/shard_map/all_to_all | solution.py:301
  14.5 4.0 %whiten.1 = (bf16[2,8320]{1,0:T(2,128)(2,1)}, bf16[16,2,8320]{2,1,0:T(2,128)(2,1)}) custom-call(s32[2]{0:T(128)} %alive.1, s32[2]{0:T(128)} %starts.1, s32[2]{0:T(128)} %halves.1, f32[128,128]{1,0:T(8,128)} %bitcast.8, bf16[256,128]{1,0:T(8,128)(2,1)} %constant.58.clone.first_h, bf16[256,128]{1,0:T(8,128)(2,1)} %constant.59.clone.first_l, ...), custom_call_target="tpu_custom_call" | custom-call | tf_op jit(solution)/shard_map/whiten/pallas_call | solution.py:171
  18.5 5.9 %collective-permute-start.1 = (bf16[1,2,8320]{2,1,0:T(2,128)(2,1)}, bf16[1,2,8320]{2,1,0:T(2,128)(2,1)S(1)}, u32[]{:S(2)}, u32[]{:S(2)}) collective-permute-start(bf16[1,2,8320]{2,1,0:T(2,128)(2,1)} %bitcast.9), channel_id=1, source_target_pairs={{0,224},{32,0},{64,32},{96,64},{128,96},{160,128},{192,160},{224,1... | collective-permute-start | bytes 99848 | tf_op jit(solution)/shard_map/ppermute | solution.py:295
  24.4 0.0 collective-permute-start
  24.4 1.9 %collective-permute-done.1 = bf16[1,2,8320]{2,1,0:T(2,128)(2,1)S(1)} collective-permute-done((bf16[1,2,8320]{2,1,0:T(2,128)(2,1)}, bf16[1,2,8320]{2,1,0:T(2,128)(2,1)S(1)}, u32[]{:S(2)}, u32[]{:S(2)}) %collective-permute-start.1) | collective-permute-done | bytes 33312 | tf_op jit(solution)/shard_map/ppermute | solution.py:295
  26.3 3.4 %collective-permute-done = bf16[1,2,8320]{2,1,0:T(2,128)(2,1)S(1)} collective-permute-done((bf16[1,2,8320]{2,1,0:T(2,128)(2,1)}, bf16[1,2,8320]{2,1,0:T(2,128)(2,1)S(1)}, u32[]{:S(2)}, u32[]{:S(2)}) %collective-permute-start) | collective-permute-done | bytes 33312 | tf_op jit(solution)/shard_map/ppermute | solution.py:295
  29.7 0.9 %pad_maximum_fusion.1.rest_0_ = bf16[3,2,8320]{2,1,0:T(2,128)(2,1)S(1)} fusion(bf16[1,2,8320]{2,1,0:T(2,128)(2,1)S(1)} %collective-permute-done.1, bf16[1,2,8320]{2,1,0:T(2,128)(2,1)S(1)} %collective-permute-done, bf16[1,2,8320]{2,1,0:T(2,128)(2,1)} %bitcast.11), kind=kLoop, calls=%fused_computation.3 | loop fusion | flops 99840 | bytes 199680 | tf_op jit(solution)/shard_map/concatenate | solution.py:306
  30.6 0.1 collective-permute-start.2
  30.7 0.0 copy-done
  30.7 0.1 pad_maximum_fusion.2
  30.9 5.1 %collective-permute-start.3 = (bf16[2,2,8320]{2,1,0:T(2,128)(2,1)S(1)}, bf16[2,2,8320]{2,1,0:T(2,128)(2,1)S(1)}, u32[]{:S(2)}, u32[]{:S(2)}) collective-permute-start(bf16[2,2,8320]{2,1,0:T(2,128)(2,1)S(1)} %pad_maximum_fusion.2), channel_id=1, source_target_pairs={{0,160},{32,192},{64,224},{96,0},{128,32},{160,64},{192,96},{224,1... | collective-permute-start | bytes 199688 | tf_op jit(solution)/shard_map/ppermute | solution.py:295
  35.9 4.9 %all-to-all-start.1 = ((bf16[16,2,8320]{2,1,0:T(2,128)(2,1)}), bf16[16,2,8320]{2,1,0:T(2,128)(2,1)S(1)}, u32[]{:S(2)}, u32[]{:S(2)}) async-start(bf16[16,2,8320]{2,1,0:T(2,128)(2,1)} %get-tuple-element.7), calls=%async_computation.1 | async-start | bytes 1064960 | tf_op jit(solution)/shard_map/all_to_all | solution.py:303
  40.8 0.0 collective-permute-done.3.rest_2_
  40.8 0.0 collective-permute-done.2.rest_1_
  40.8 0.2 pad_maximum_fusion
  41.1 0.1 collective-permute-start.5
  41.2 0.5 collective-permute-start.4
  41.6 1.0 %collective-permute-done.4.rest_3_ = bf16[3,2,8320]{2,1,0:T(2,128)(2,1)S(1)} collective-permute-done((bf16[3,2,8320]{2,1,0:T(2,128)(2,1)S(1)}, bf16[3,2,8320]{2,1,0:T(2,128)(2,1)S(1)}, u32[]{:S(2)}, u32[]{:S(2)}) %collective-permute-start.4) | collective-permute-done | bytes 99872 | tf_op jit(solution)/shard_map/ppermute | solution.py:295
  42.7 0.0 collective-permute-done.5.rest_4_
  42.7 7.0 %all-to-all-done.1.rows_ref = bf16[16,2,8320]{2,1,0:T(2,128)(2,1)S(1)} async-done(((bf16[16,2,8320]{2,1,0:T(2,128)(2,1)}), bf16[16,2,8320]{2,1,0:T(2,128)(2,1)S(1)}, u32[]{:S(2)}, u32[]{:S(2)}) %all-to-all-start.1) | async-done | bytes 532512 | tf_op jit(solution)/shard_map/all_to_all | solution.py:303
  49.7 6.5 %correlate.1 = bf16[16,72,128]{2,1,0:T(8,128)(2,1)} custom-call(bf16[16,2,8320]{2,1,0:T(2,128)(2,1)S(1)} %all-to-all-done.1.rows_ref, bf16[3,2,8320]{2,1,0:T(2,128)(2,1)S(1)} %pad_maximum_fusion.1.rest_0_, bf16[3,2,8320]{2,1,0:T(2,128)(2,1)S(1)} %collective-permute-done.2.rest_1_, bf16[2,2,8320]{2,1,0:T(2,128)(2,1)S(1)} %collective-permute-done.3.rest_2_, ...), custom_call_target="tpu_custom_call" | custom-call | flops 2453667840 | bytes 4194304 | tf_op jit(solution)/shard_map/correlate/pallas_call | solution.py:228
  56.2 0.0 copy-start.1
  56.2 0.0 copy-start.2
  56.2 0.0 copy-start.3
  56.2 5.0 %all-to-all-start.2 = ((bf16[16,72,128]{2,1,0:T(8,128)(2,1)}), bf16[16,72,128]{2,1,0:T(8,128)(2,1)S(1)}, u32[]{:S(2)}, u32[]{:S(2)}) async-start(bf16[16,72,128]{2,1,0:T(8,128)(2,1)} %correlate.1), calls=%async_computation.2 | async-start | bytes 589824 | tf_op jit(solution)/shard_map/all_to_all | solution.py:312
  61.1 0.0 copy-done.1
  61.1 0.0 copy-done.2
  61.2 0.0 copy-done.3
  61.2 0.2 fusion.perm_ref
  61.4 7.4 %all-to-all-done.2.x_ref = bf16[16,72,128]{2,1,0:T(8,128)(2,1)S(1)} async-done(((bf16[16,72,128]{2,1,0:T(8,128)(2,1)}), bf16[16,72,128]{2,1,0:T(8,128)(2,1)S(1)}, u32[]{:S(2)}, u32[]{:S(2)}) %all-to-all-start.2) | async-done | bytes 294944 | tf_op jit(solution)/shard_map/all_to_all | solution.py:312
  68.7 1.4 %place.1 = bf16[129,2,512]{2,1,0:T(2,128)(2,1)} custom-call(s32[1]{0:T(128)} %bitcast.own, bf16[16,72,128]{2,1,0:T(8,128)(2,1)S(1)} %all-to-all-done.2.x_ref, bf16[512,512]{1,0:T(8,128)(2,1)S(1)} %fusion.perm_ref), custom_call_target="tpu_custom_call" | custom-call | tf_op jit(solution)/shard_map/place/pallas_call | solution.py:278
  (3 shorter events, 0.0 us)
Async XLA Ops:
  18.5 12.2 %copy-start = (bf16[2,8320]{1,0:T(2,128)(2,1)S(1)}, bf16[2,8320]{1,0:T(2,128)(2,1)}, u32[]{:S(2)}) copy-start(bf16[2,8320]{1,0:T(2,128)(2,1)} %get-tuple-element.8) | copy-start | bytes 99844
  18.5 7.8 %collective-permute-start.1 = (bf16[1,2,8320]{2,1,0:T(2,128)(2,1)}, bf16[1,2,8320]{2,1,0:T(2,128)(2,1)S(1)}, u32[]{:S(2)}, u32[]{:S(2)}) collective-permute-start(bf16[1,2,8320]{2,1,0:T(2,128)(2,1)} %bitcast.9), channel_id=1, source_target_pairs={{0,224},{32,0},{64,32},{96,64},{128,96},{160,128},{192,160},{224,1... | collective-permute-start | bytes 99848 | tf_op jit(solution)/shard_map/ppermute | solution.py:295
  24.4 5.3 %collective-permute-start = (bf16[1,2,8320]{2,1,0:T(2,128)(2,1)}, bf16[1,2,8320]{2,1,0:T(2,128)(2,1)S(1)}, u32[]{:S(2)}, u32[]{:S(2)}) collective-permute-start(bf16[1,2,8320]{2,1,0:T(2,128)(2,1)} %bitcast.10), channel_id=1, source_target_pairs={{0,32},{32,64},{64,96},{96,128},{128,160},{160,192},{192,224},{224... | collective-permute-start | bytes 99848 | tf_op jit(solution)/shard_map/ppermute | solution.py:295
  30.6 10.2 %collective-permute-start.2 = (bf16[3,2,8320]{2,1,0:T(2,128)(2,1)S(1)}, bf16[3,2,8320]{2,1,0:T(2,128)(2,1)S(1)}, u32[]{:S(2)}, u32[]{:S(2)}) collective-permute-start(bf16[3,2,8320]{2,1,0:T(2,128)(2,1)S(1)} %pad_maximum_fusion.1.rest_0_), channel_id=1, source_target_pairs={{0,96},{32,128},{64,160},{96,192},{128,224},{160,0},{192,32},{224,... | collective-permute-start | bytes 299528 | tf_op jit(solution)/shard_map/ppermute | solution.py:295
  30.9 10.0 %collective-permute-start.3 = (bf16[2,2,8320]{2,1,0:T(2,128)(2,1)S(1)}, bf16[2,2,8320]{2,1,0:T(2,128)(2,1)S(1)}, u32[]{:S(2)}, u32[]{:S(2)}) collective-permute-start(bf16[2,2,8320]{2,1,0:T(2,128)(2,1)S(1)} %pad_maximum_fusion.2), channel_id=1, source_target_pairs={{0,160},{32,192},{64,224},{96,0},{128,32},{160,64},{192,96},{224,1... | collective-permute-start | bytes 199688 | tf_op jit(solution)/shard_map/ppermute | solution.py:295
  35.9 13.7 %all-to-all-start.1 = ((bf16[16,2,8320]{2,1,0:T(2,128)(2,1)}), bf16[16,2,8320]{2,1,0:T(2,128)(2,1)S(1)}, u32[]{:S(2)}, u32[]{:S(2)}) async-start(bf16[16,2,8320]{2,1,0:T(2,128)(2,1)} %get-tuple-element.7), calls=%async_computation.1 | async-start | bytes 1064960 | tf_op jit(solution)/shard_map/all_to_all | solution.py:303
  41.1 1.6 %collective-permute-start.5 = (bf16[5,2,8320]{2,1,0:T(2,128)(2,1)S(1)}, bf16[5,2,8320]{2,1,0:T(2,128)(2,1)S(1)}, u32[]{:S(2)}, u32[]{:S(2)}) collective-permute-start(bf16[5,2,8320]{2,1,0:T(2,128)(2,1)S(1)} %pad_maximum_fusion), channel_id=1, source_target_pairs={{0,1},{1,0},{2,3},{3,2},{4,5},{5,4},{6,7},{7,6},{8,9},{9,8},{10,11... | collective-permute-start | bytes 499208 | tf_op jit(solution)/shard_map/ppermute | solution.py:295
  41.2 1.5 %collective-permute-start.4 = (bf16[3,2,8320]{2,1,0:T(2,128)(2,1)S(1)}, bf16[3,2,8320]{2,1,0:T(2,128)(2,1)S(1)}, u32[]{:S(2)}, u32[]{:S(2)}) collective-permute-start(bf16[3,2,8320]{2,1,0:T(2,128)(2,1)S(1)} %pad_maximum_fusion.1.rest_0_), channel_id=1, source_target_pairs={{0,1},{1,0},{2,3},{3,2},{4,5},{5,4},{6,7},{7,6},{8,9},{9,8},{10,11... | collective-permute-start | bytes 299528 | tf_op jit(solution)/shard_map/ppermute | solution.py:295
  56.2 5.0 %copy-start.1 = (s32[512]{0:T(512)S(1)}, s32[512]{0:T(512)}, u32[]{:S(2)}) copy-start(s32[512]{0:T(512)} %constant.70.clone) | copy-start | bytes 6148
  56.2 5.0 %copy-start.2 = (s32[512]{0:T(512)S(1)}, s32[512]{0:T(512)}, u32[]{:S(2)}) copy-start(s32[512]{0:T(512)} %constant.69.clone) | copy-start | bytes 6148
  56.2 5.0 %copy-start.3 = (s32[512]{0:T(512)S(1)}, s32[512]{0:T(512)}, u32[]{:S(2)}) copy-start(s32[512]{0:T(512)} %constant.68.clone) | copy-start | bytes 6148
  56.2 12.6 %all-to-all-start.2 = ((bf16[16,72,128]{2,1,0:T(8,128)(2,1)}), bf16[16,72,128]{2,1,0:T(8,128)(2,1)S(1)}, u32[]{:S(2)}, u32[]{:S(2)}) async-start(bf16[16,72,128]{2,1,0:T(8,128)(2,1)} %correlate.1), calls=%async_computation.2 | async-start | bytes 589824 | tf_op jit(solution)/shard_map/all_to_all | solution.py:312

commit v3 on v2

--- a/solution.py
+++ b/solution.py
@@ -55,10 +55,10 @@
     ], axis=0)
     out = []
     for table in (first, second, third, last):
-        out.extend(split_const(table))
+        for piece in split_const(table):
+            out.extend(piece[:, at:at + 128] for at in range(0, piece.shape[1], 128))
     out.append(tri.astype(ml_dtypes.bfloat16))
-    out.append(twiddle.astype(np.float32))
-    return out
+    return [np.concatenate(out, axis=0), twiddle.astype(np.float32)]
 
 
 def parts2(x):
@@ -87,8 +87,7 @@
     return dot(high, xh) + (dot(high, xl) + dot(low, xh))
 
 
-def whiten_kernel(alive, starts, halves, x_ref, first_h, first_l, second_h, second_l, third_h, third_l,
-                  last_h, last_l, tri_ref, twid_ref, out_ref, spread_ref, sig, pad):
+def whiten_kernel(alive, starts, halves, x_ref, mats, twid_ref, out_ref, spread_ref, sig, pad):
     lane = lax.broadcasted_iota(jnp.int32, (Q, 128), 1)
     sig[...] = jnp.zeros_like(sig)
     pad[...] = jnp.zeros_like(pad)
@@ -124,17 +123,21 @@
         level = total / (2 * half + 1).astype(f32)
         normed.append(signal / (level + TINY))
     x = jnp.concatenate(normed, axis=0)
+    first_h, first_l, second_h, second_l = (mats[k * 256:(k + 1) * 256, :] for k in range(4))
+    third_h, third_l, last_h, last_l = (
+        jnp.concatenate([mats[k * 256:k * 256 + 128, :], mats[k * 256 + 128:(k + 1) * 256, :]], axis=1)
+        for k in range(4, 8))
     cos_t = twid_ref[0:128, :]
     sin_t = twid_ref[128:256, :]
-    stage = left_product(first_h[...], first_l[...], x)
+    stage = left_product(first_h, first_l, x)
     re, im = stage[0:128], stage[128:256]
     turned = jnp.concatenate([re * cos_t + im * sin_t, im * cos_t - re * sin_t], axis=1)
-    spec = right_product(turned, second_h[...], second_l[...])
+    spec = right_product(turned, second_h, second_l)
     square = spec * spec
     size = jnp.sqrt(square + pltpu.roll(square, BINS, 1))
     sums = None
     for term in parts3(size):
-        add = dot(tri_ref[...], term)
+        add = dot(mats[2048:2432, :], term)
         sums = add if sums is None else sums + add
     smooth = (sums[0:128] + pltpu.roll(sums[128:256], 1, 1) + pltpu.roll(sums[256:384], 127, 1)) / 65.0
     k1 = lax.broadcasted_iota(jnp.int32, (128, 128), 0) % Q
@@ -142,10 +145,10 @@
     bins = k1 + Q * (jj - 1)
     band = (bins >= BAND_LO) & (bins <= BAND_HI)
     gain = jnp.where(band, 2.0 / math.sqrt(NT), 0.0) / (smooth + TINY)
-    stage = right_product(spec * gain, third_h[...], third_l[...])
+    stage = right_product(spec * gain, third_h, third_l)
     re, im = stage[:, 0:128], stage[:, 128:256]
     turned = jnp.concatenate([re * cos_t - im * sin_t, im * cos_t + re * sin_t], axis=0)
-    white = left_product(last_h[...], last_l[...], turned)
+    white = left_product(last_h, last_l, turned)
     rolled = pltpu.roll(white, 64, 1)
     for r in range(2):
         sig[pl.ds(r * 40, Q), :] = white[r * 64:r * 64 + Q]
@@ -171,7 +174,7 @@
     return pl.pallas_call(
         whiten_kernel,
         out_shape=(jax.ShapeDtypeStruct((2, LINE), bf16), jax.ShapeDtypeStruct((16, 2, LINE), bf16)),
-        in_specs=[smem] * 3 + [vmem] * (1 + len(consts)),
+        in_specs=[smem] * 3 + [vmem] * 3,
         out_specs=(vmem, vmem),
         scratch_shapes=[pltpu.VMEM((4 * 48, 128), f32), pltpu.VMEM((4 * 48, 128), f32)],
         name="whiten",
@@ -189,17 +192,23 @@
 
 
 def corr_kernel(rows_ref, *rest):
-    cols, (out_ref, xi, xj, acc, left, right, tall, form) = rest[:-8], rest[-8:]
+    cols, (out_ref, held, sems, xi, xj, acc, left0, right0, left1, right1, tall, form) = rest[:-12], rest[-12:]
+    copies, at = [], 0
+    for k, ref in enumerate(cols):
+        copies.append(pltpu.make_async_copy(ref, held.at[at:at + ref.shape[0]], sems.at[k]))
+        copies[-1].start()
+        at += ref.shape[0]
     load_lines([rows_ref], xi)
-    load_lines(cols, xj)
-    acc[...] = jnp.zeros_like(acc)
-
-    @pl.loop(0, LINE // CHUNK)
-    def _(step):
-        at = pl.multiple_of(step * CHUNK, 128)
-        wide = CHUNK + 256
-        line_i = xi[:, pl.ds(at, wide)]
-        line_j = xj[:, pl.ds(at, wide)]
+    for copy in copies:
+        copy.wait()
+    load_lines([held], xj)
+    wide = CHUNK + 256
+    slots = ((left0, right0), (left1, right1))
+
+    def expand(step):
+        left, right = slots[step % 2]
+        line_i = xi[:, step * CHUNK:step * CHUNK + wide]
+        line_j = xj[:, step * CHUNK:step * CHUNK + wide]
         for a in range(A_BLOCKS + 1):
             shift = (STEP * a - LAG) % wide
             moved = pltpu.roll(line_i, shift, 1) if shift else line_i
@@ -207,7 +216,14 @@
         for b in range(STEP):
             moved = pltpu.roll(line_j, wide - b, 1) if b else line_j
             right[b * 32:(b + 1) * 32, :] = moved[:, 128:128 + CHUNK]
-        acc[...] += lax.dot_general(left[...], right[...], (((1,), (1,)), ((), ())), preferred_element_type=f32)
+
+    expand(0)
+    for step in range(LINE // CHUNK):
+        if step + 1 < LINE // CHUNK:
+            expand(step + 1)
+        left, right = slots[step % 2]
+        add = lax.dot_general(left[...], right[...], (((1,), (1,)), ((), ())), preferred_element_type=f32)
+        acc[...] = add if step == 0 else acc[...] + add
 
     scale = 1.0 / math.sqrt(2 * NT)
     for bh in range(4):
@@ -228,11 +244,13 @@
     return pl.pallas_call(
         corr_kernel,
         out_shape=jax.ShapeDtypeStruct((16, 72, 128), bf16),
-        in_specs=[vmem] * (1 + len(cols_in)),
+        in_specs=[vmem] + [pl.BlockSpec(memory_space=pl.ANY)] * len(cols_in),
         out_specs=vmem,
         scratch_shapes=[
+            pltpu.VMEM((16, 2, LINE), bf16), pltpu.SemaphoreType.DMA((len(cols_in),)),
             pltpu.VMEM((32, LINE + 256), bf16), pltpu.VMEM((32, LINE + 256), bf16),
             pltpu.VMEM((rows, cols), f32), pltpu.VMEM((rows, CHUNK), bf16), pltpu.VMEM((cols, CHUNK), bf16),
+            pltpu.VMEM((rows, CHUNK), bf16), pltpu.VMEM((cols, CHUNK), bf16),
             pltpu.VMEM((4 * rows, 128), f32), pltpu.VMEM((72, 128), f32),
         ],
         compiler_params=pltpu.CompilerParams(vmem_limit_bytes=32 << 20),
@@ -290,9 +308,23 @@
 SLABS = ("x", "yh", "core")
 
 
-def passed(value, axis, by):
-    length = lax.axis_size(axis)
-    return lax.ppermute(value, axis, [(i, (i + by) % length) for i in range(length)])
+def crossed(value):
+    return lax.ppermute(value, "core", [(0, 1), (1, 0)])
+
+
+def shed(value, by):
+    pairs = []
+    for z in range(8):
+        pairs.append((z * 2, (z + by) % 8 * 2))
+        pairs.append((z * 2 + 1, (z - by) % 8 * 2 + 1))
+    return lax.ppermute(value, ("z", "core"), pairs)
+
+
+def columns_by_hops(pair):
+    one = shed(pair, 1)
+    more = shed(jnp.concatenate([pair, one], axis=0), 2)
+    four = shed(more[2:4], 1)
+    return one, more, four, crossed(one), crossed(more)
 
 
 def on_device(raw, alive, seg_start, norm_half):
@@ -302,20 +334,16 @@
     white, spread = whiten(traces, alive, seg_start, norm_half)
     rows = lax.all_to_all(spread, PLANE, split_axis=0, concat_axis=0, tiled=True)
     white = white[None]
-    up, down = passed(white, "z", 1), passed(white, "z", -1)
-    near = jnp.concatenate([white, up, down], axis=0)
-    far_up = passed(near, "z", 3)
-    far_down = passed(jnp.concatenate([white, up], axis=0), "z", -3)
-    near_other = passed(near, "core", 1)
-    far_other = passed(jnp.concatenate([far_up, far_down], axis=0), "core", 1)
-    block = correlate(rows, [near, far_up, far_down, near_other, far_other])
+    pair = jnp.concatenate([white, crossed(white)], axis=0)
+    block = correlate(rows, (pair,) + columns_by_hops(pair))
     back = lax.all_to_all(block, PLANE, split_axis=0, concat_axis=0, tiled=True)
     k = np.arange(512)
-    e, half, j = k // 32, (k // 16) % 2, k % 16
-    offset = np.repeat([0, 7, 1, 5, 4, 6, 3, 2], 2)[j]
-    fixed = (e // 8) * 32 + ((e // 2) % 4) * 8 + (e % 2) * 4 + j % 2
-    from_z = (z + jnp.asarray(offset, jnp.int32)) & 7
-    target = from_z * 64 + jnp.asarray(fixed, jnp.int32) + (core ^ jnp.asarray(half, jnp.int32)) * 2
+    e, pair_id, side = k // 32, (k // 4) % 8, (k // 2) % 2
+    step = np.array([0, 1, 2, 3, 4, -1, -2, -3])[pair_id]
+    side = side ^ (pair_id >= 5)
+    fixed = (e // 8) * 32 + ((e // 2) % 4) * 8 + (e % 2) * 4 + k % 2
+    from_z = (z + jnp.asarray(step, jnp.int32) * (2 * core - 1)) & 7
+    target = from_z * 64 + jnp.asarray(fixed, jnp.int32) + (core ^ jnp.asarray(side, jnp.int32)) * 2
     k = lax.iota(jnp.int32, 512)
     perm = (target[:, None] == k[None, :]).astype(bf16)
     own = (((z * 2 + yl) * 16 + x * 4 + yh * 2 + core) * 2).astype(jnp.int32).reshape(1)

time: 70.6 us -> 66.8 us (0.946)
  starting transfers between devices: 21.5 us -> 17.4 us
  waiting for transfers between devices: 20.7 us -> 21.8 us
    ppermute x6, waiting for transfers between devices: 6.38 us -> 14.4 us  [the longest x3 12.4 us: shed(): return lax.ppermute(value, ('z', 'core'), pairs)]
    all_to_all x1, waiting for transfers between devices: 6.97 us -> 0.01 us  [on_device(): lax.all_to_all(spread, PLANE, split_axis=0, concat_axis=0, tiled=True)]
    ppermute x6, starting transfers between devices: 11.6 us -> 4.99 us  [the longest x3 4.37 us: shed(): return lax.ppermute(value, ('z', 'core'), pairs)]
    all_to_all x1, starting transfers between devices: 4.97 us -> 7.39 us  [on_device(): back = lax.all_to_all(block, PLANE, split_axis=0, concat_axis=0, tiled=True)]
  transfers between devices with their start and end apart: 8 -> 8, of which waited for: 5 -> 6; matrix products, arithmetic and copies ran while one was open for 1% -> 1% of each run, Pallas kernels for 0% -> 0%
where the time goes in v3:
time: 66.8 us; the launch traced here: 66.3 us
  waiting for transfers between devices  21.8 us (33%)
  starting transfers between devices  17.4 us (26%)
  blocking collectives  13.6 us (20%)
  Pallas kernels  11.2 us (17%)
  other arithmetic  1.21 us (2%)
  local copies, waits for them, and re-layouts  0.96 us (1%)
    all_to_all x1, blocking collectives, on_device(): lax.all_to_all(sent, SLABS, split_axis=0, concat_axis=0, tiled=True)  13.6 us
    ppermute x3, waiting for transfers between devices, shed(): return lax.ppermute(value, ('z', 'core'), pairs)  12.4 us
    all_to_all x1, starting transfers between devices, on_device(): back = lax.all_to_all(block, PLANE, split_axis=0, concat_axis=0, tiled=True)  7.39 us
    all_to_all x1, waiting for transfers between devices, on_device(): back = lax.all_to_all(block, PLANE, split_axis=0, concat_axis=0, tiled=True)  7.38 us
    pallas_call x1, Pallas kernels, correlate(): pl.pallas_call(corr_kernel, out_shape=jax.ShapeDtypeStruct((16, 72, 128),...  5.99 us
    all_to_all x1, starting transfers between devices, on_device(): lax.all_to_all(spread, PLANE, split_axis=0, concat_axis=0, tiled=True)  5 us
    ppermute x3, starting transfers between devices, shed(): return lax.ppermute(value, ('z', 'core'), pairs)  4.37 us
    pallas_call x1, Pallas kernels, whiten(): pl.pallas_call(whiten_kernel, out_shape=(jax.ShapeDtypeStruct((2, LINE),...  3.87 us
  transfers between devices with their start and end apart: 8, of which 6 were waited for; matrix products, arithmetic and copies ran while one was open for 1% of the time, Pallas kernels for 0%

profile of v3, /device:TPU:2, one launch (start us, length us, event | category | flops | bytes accessed | tf_op | source)
XLA Modules:
  0.0 66.3 jit_solution(6881198471310155240)
XLA Ops:
  0.0 0.9 %reshape.14 = f32[2,16,2,2,128]{4,3,2,1,0:T(2,128)S(1)} reshape(f32[2,32,256]{2,1,0:T(8,128)} %param.9) | data formatting | bytes 131072 | tf_op jit(solution)/shard_map/reshape | solution.py:332
  0.9 13.6 %all_to_all.15 = f32[16,8,128]{2,1,0:T(8,128)} all-to-all(f32[16,8,128]{2,1,0:T(8,128)S(1)} %bitcast.6), channel_id=1, replica_groups=mesh['z'=8,'yl'=2,'x'=4,'yh'=2,'core'=2] {'x','yh','core'}, dimensions={0} | all-to-all | bytes 131072 | tf_op jit(solution)/shard_map/all_to_all | solution.py:333
  14.5 3.9 %whiten.1 = (bf16[2,8320]{1,0:T(2,128)(2,1)}, bf16[16,2,8320]{2,1,0:T(2,128)(2,1)}) custom-call(s32[2]{0:T(128)} %alive.1, s32[2]{0:T(128)} %starts.1, s32[2]{0:T(128)} %halves.1, f32[128,128]{1,0:T(8,128)} %bitcast.8, bf16[2432,128]{1,0:T(8,128)(2,1)} %constant.45.clone.mats, f32[256,128]{1,0:T(8,128)} %constant.46.clone.twid_ref), custom_call_target="tpu_custom_call" | custom-call | tf_op jit(solution)/shard_map/whiten/pallas_call | solution.py:174
  18.4 0.1 collective-permute-start
  18.5 1.3 %collective-permute-done = bf16[1,2,8320]{2,1,0:T(2,128)(2,1)S(1)} collective-permute-done((bf16[1,2,8320]{2,1,0:T(2,128)(2,1)}, bf16[1,2,8320]{2,1,0:T(2,128)(2,1)S(1)}, u32[]{:S(2)}, u32[]{:S(2)}) %collective-permute-start) | collective-permute-done | bytes 33312 | tf_op jit(solution)/shard_map/ppermute | solution.py:312
  19.8 0.9 %pad_maximum_fusion.1.rest_0_ = bf16[2,2,8320]{2,1,0:T(2,128)(2,1)S(1)} fusion(bf16[1,2,8320]{2,1,0:T(2,128)(2,1)S(1)} %collective-permute-done, bf16[1,2,8320]{2,1,0:T(2,128)(2,1)} %bitcast.10), kind=kLoop, calls=%fused_computation.3 | loop fusion | flops 33280 | bytes 133120 | tf_op jit(solution)/shard_map/concatenate | solution.py:337
  20.7 2.0 %collective-permute-start.1 = (bf16[2,2,8320]{2,1,0:T(2,128)(2,1)S(1)}, bf16[2,2,8320]{2,1,0:T(2,128)(2,1)S(1)}, u32[]{:S(2)}, u32[]{:S(2)}) collective-permute-start(bf16[2,2,8320]{2,1,0:T(2,128)(2,1)S(1)} %pad_maximum_fusion.1.rest_0_), channel_id=1, source_target_pairs={{0,32},{1,225},{32,64},{33,1},{64,96},{65,33},{96,128},{97,65},{12... | collective-permute-start | bytes 199688 | tf_op jit(solution)/shard_map/ppermute | solution.py:320
  22.7 0.0 copy-start
  22.7 5.0 %all-to-all-start.1 = ((bf16[16,2,8320]{2,1,0:T(2,128)(2,1)}), bf16[16,2,8320]{2,1,0:T(2,128)(2,1)S(1)}, u32[]{:S(2)}, u32[]{:S(2)}) async-start(bf16[16,2,8320]{2,1,0:T(2,128)(2,1)} %get-tuple-element.7), calls=%async_computation.1 | async-start | bytes 1064960 | tf_op jit(solution)/shard_map/all_to_all | solution.py:335
  27.7 1.2 %collective-permute-done.1.rest_1_ = bf16[2,2,8320]{2,1,0:T(2,128)(2,1)S(1)} collective-permute-done((bf16[2,2,8320]{2,1,0:T(2,128)(2,1)S(1)}, bf16[2,2,8320]{2,1,0:T(2,128)(2,1)S(1)}, u32[]{:S(2)}, u32[]{:S(2)}) %collective-permute-start.1) | collective-permute-done | bytes 66592 | tf_op jit(solution)/shard_map/ppermute | solution.py:320
  28.9 0.0 copy-done
  28.9 0.2 pad_maximum_fusion
  29.1 2.2 %collective-permute-start.2 = (bf16[4,2,8320]{2,1,0:T(2,128)(2,1)S(1)}, bf16[4,2,8320]{2,1,0:T(2,128)(2,1)S(1)}, u32[]{:S(2)}, u32[]{:S(2)}) collective-permute-start(bf16[4,2,8320]{2,1,0:T(2,128)(2,1)S(1)} %pad_maximum_fusion), channel_id=1, source_target_pairs={{0,64},{1,193},{32,96},{33,225},{64,128},{65,1},{96,160},{97,33},{... | collective-permute-start | bytes 399368 | tf_op jit(solution)/shard_map/ppermute | solution.py:320
  31.2 6.5 %collective-permute-done.2.rest_2_ = bf16[4,2,8320]{2,1,0:T(2,128)(2,1)S(1)} collective-permute-done((bf16[4,2,8320]{2,1,0:T(2,128)(2,1)S(1)}, bf16[4,2,8320]{2,1,0:T(2,128)(2,1)S(1)}, u32[]{:S(2)}, u32[]{:S(2)}) %collective-permute-start.2) | collective-permute-done | bytes 133152 | tf_op jit(solution)/shard_map/ppermute | solution.py:320
  37.8 0.0 collective-permute-start.5
  37.8 0.5 collective-permute-start.4
  38.3 0.2 collective-permute-start.3
  38.5 0.7 %collective-permute-done.4.rest_4_ = bf16[2,2,8320]{2,1,0:T(2,128)(2,1)S(1)} collective-permute-done((bf16[2,2,8320]{2,1,0:T(2,128)(2,1)S(1)}, bf16[2,2,8320]{2,1,0:T(2,128)(2,1)S(1)}, u32[]{:S(2)}, u32[]{:S(2)}) %collective-permute-start.4) | collective-permute-done | bytes 66592 | tf_op jit(solution)/shard_map/ppermute | solution.py:312
  39.2 4.7 %collective-permute-done.3.rest_3_ = bf16[2,2,8320]{2,1,0:T(2,128)(2,1)S(1)} collective-permute-done((bf16[2,2,8320]{2,1,0:T(2,128)(2,1)S(1)}, bf16[2,2,8320]{2,1,0:T(2,128)(2,1)S(1)}, u32[]{:S(2)}, u32[]{:S(2)}) %collective-permute-start.3) | collective-permute-done | bytes 66592 | tf_op jit(solution)/shard_map/ppermute | solution.py:320
  43.9 0.0 collective-permute-done.5.rest_5_
  43.9 0.0 all-to-all-done.1.rows_ref
  43.9 6.0 %correlate.1 = bf16[16,72,128]{2,1,0:T(8,128)(2,1)} custom-call(bf16[16,2,8320]{2,1,0:T(2,128)(2,1)S(1)} %all-to-all-done.1.rows_ref, bf16[2,2,8320]{2,1,0:T(2,128)(2,1)S(1)} %pad_maximum_fusion.1.rest_0_, bf16[2,2,8320]{2,1,0:T(2,128)(2,1)S(1)} %collective-permute-done.1.rest_1_, bf16[4,2,8320]{2,1,0:T(2,128)(2,1)S(1)} %collective-permute-done.2.rest_2_, ...), custom_call_target="tpu_custom_call" | custom-call | flops 2453667840 | bytes 4194304 | tf_op jit(solution)/shard_map/correlate/pallas_call | solution.py:244
  49.9 0.0 copy-start.1
  49.9 0.0 copy-start.2
  49.9 0.0 copy-start.3
  49.9 7.4 %all-to-all-start.2 = ((bf16[16,72,128]{2,1,0:T(8,128)(2,1)}), bf16[16,72,128]{2,1,0:T(8,128)(2,1)S(1)}, u32[]{:S(2)}, u32[]{:S(2)}) async-start(bf16[16,72,128]{2,1,0:T(8,128)(2,1)} %correlate.1), calls=%async_computation.2 | async-start | bytes 589824 | tf_op jit(solution)/shard_map/all_to_all | solution.py:339
  57.3 0.0 copy-done.1
  57.3 0.0 copy-done.2
  57.3 0.0 copy-done.3
  57.4 0.2 fusion.perm_ref
  57.5 7.4 %all-to-all-done.2.x_ref = bf16[16,72,128]{2,1,0:T(8,128)(2,1)S(1)} async-done(((bf16[16,72,128]{2,1,0:T(8,128)(2,1)}), bf16[16,72,128]{2,1,0:T(8,128)(2,1)S(1)}, u32[]{:S(2)}, u32[]{:S(2)}) %all-to-all-start.2) | async-done | bytes 294944 | tf_op jit(solution)/shard_map/all_to_all | solution.py:339
  64.9 1.4 %place.1 = bf16[129,2,512]{2,1,0:T(2,128)(2,1)} custom-call(s32[1]{0:T(128)} %bitcast.own, bf16[16,72,128]{2,1,0:T(8,128)(2,1)S(1)} %all-to-all-done.2.x_ref, bf16[512,512]{1,0:T(8,128)(2,1)S(1)} %fusion.perm_ref), custom_call_target="tpu_custom_call" | custom-call | tf_op jit(solution)/shard_map/place/pallas_call | solution.py:296
  (3 shorter events, 0.1 us)
Async XLA Ops:
  18.4 1.4 %collective-permute-start = (bf16[1,2,8320]{2,1,0:T(2,128)(2,1)}, bf16[1,2,8320]{2,1,0:T(2,128)(2,1)S(1)}, u32[]{:S(2)}, u32[]{:S(2)}) collective-permute-start(bf16[1,2,8320]{2,1,0:T(2,128)(2,1)} %bitcast.9), channel_id=1, source_target_pairs={{0,1},{1,0},{2,3},{3,2},{4,5},{5,4},{6,7},{7,6},{8,9},{9,8},{10,11... | collective-permute-start | bytes 99848 | tf_op jit(solution)/shard_map/ppermute | solution.py:312
  20.7 8.2 %collective-permute-start.1 = (bf16[2,2,8320]{2,1,0:T(2,128)(2,1)S(1)}, bf16[2,2,8320]{2,1,0:T(2,128)(2,1)S(1)}, u32[]{:S(2)}, u32[]{:S(2)}) collective-permute-start(bf16[2,2,8320]{2,1,0:T(2,128)(2,1)S(1)} %pad_maximum_fusion.1.rest_0_), channel_id=1, source_target_pairs={{0,32},{1,225},{32,64},{33,1},{64,96},{65,33},{96,128},{97,65},{12... | collective-permute-start | bytes 199688 | tf_op jit(solution)/shard_map/ppermute | solution.py:320
  22.7 6.2 %copy-start = (bf16[2,8320]{1,0:T(2,128)(2,1)S(1)}, bf16[2,8320]{1,0:T(2,128)(2,1)}, u32[]{:S(2)}) copy-start(bf16[2,8320]{1,0:T(2,128)(2,1)} %get-tuple-element.8) | copy-start | bytes 99844
  22.7 21.2 %all-to-all-start.1 = ((bf16[16,2,8320]{2,1,0:T(2,128)(2,1)}), bf16[16,2,8320]{2,1,0:T(2,128)(2,1)S(1)}, u32[]{:S(2)}, u32[]{:S(2)}) async-start(bf16[16,2,8320]{2,1,0:T(2,128)(2,1)} %get-tuple-element.7), calls=%async_computation.1 | async-start | bytes 1064960 | tf_op jit(solution)/shard_map/all_to_all | solution.py:335
  29.1 8.7 %collective-permute-start.2 = (bf16[4,2,8320]{2,1,0:T(2,128)(2,1)S(1)}, bf16[4,2,8320]{2,1,0:T(2,128)(2,1)S(1)}, u32[]{:S(2)}, u32[]{:S(2)}) collective-permute-start(bf16[4,2,8320]{2,1,0:T(2,128)(2,1)S(1)} %pad_maximum_fusion), channel_id=1, source_target_pairs={{0,64},{1,193},{32,96},{33,225},{64,128},{65,1},{96,160},{97,33},{... | collective-permute-start | bytes 399368 | tf_op jit(solution)/shard_map/ppermute | solution.py:320
  37.8 6.1 %collective-permute-start.5 = (bf16[4,2,8320]{2,1,0:T(2,128)(2,1)S(1)}, bf16[4,2,8320]{2,1,0:T(2,128)(2,1)S(1)}, u32[]{:S(2)}, u32[]{:S(2)}) collective-permute-start(bf16[4,2,8320]{2,1,0:T(2,128)(2,1)S(1)} %collective-permute-done.2.rest_2_), channel_id=1, source_target_pairs={{0,1},{1,0},{2,3},{3,2},{4,5},{5,4},{6,7},{7,6},{8,9},{9,8},{10,11... | collective-permute-start | bytes 399368 | tf_op jit(solution)/shard_map/ppermute | solution.py:312
  37.8 1.4 %collective-permute-start.4 = (bf16[2,2,8320]{2,1,0:T(2,128)(2,1)S(1)}, bf16[2,2,8320]{2,1,0:T(2,128)(2,1)S(1)}, u32[]{:S(2)}, u32[]{:S(2)}) collective-permute-start(bf16[2,2,8320]{2,1,0:T(2,128)(2,1)S(1)} %collective-permute-done.1.rest_1_), channel_id=1, source_target_pairs={{0,1},{1,0},{2,3},{3,2},{4,5},{5,4},{6,7},{7,6},{8,9},{9,8},{10,11... | collective-permute-start | bytes 199688 | tf_op jit(solution)/shard_map/ppermute | solution.py:312
  38.3 5.6 %collective-permute-start.3 = (bf16[2,2,8320]{2,1,0:T(2,128)(2,1)S(1)}, bf16[2,2,8320]{2,1,0:T(2,128)(2,1)S(1)}, u32[]{:S(2)}, u32[]{:S(2)}) collective-permute-start(bf16[2,2,8320]{2,1,0:T(2,128)(2,1)S(1)} %slice.4), channel_id=1, source_target_pairs={{0,32},{1,225},{32,64},{33,1},{64,96},{65,33},{96,128},{97,65},{12... | collective-permute-start | bytes 199688 | tf_op jit(solution)/shard_map/ppermute | solution.py:320
  49.9 7.4 %copy-start.1 = (s32[512]{0:T(512)S(1)}, s32[512]{0:T(512)}, u32[]{:S(2)}) copy-start(s32[512]{0:T(512)} %constant.49.clone) | copy-start | bytes 6148
  49.9 7.4 %copy-start.2 = (s32[512]{0:T(512)S(1)}, s32[512]{0:T(512)}, u32[]{:S(2)}) copy-start(s32[512]{0:T(512)} %constant.48.clone) | copy-start | bytes 6148
  49.9 7.4 %copy-start.3 = (s32[512]{0:T(512)S(1)}, s32[512]{0:T(512)}, u32[]{:S(2)}) copy-start(s32[512]{0:T(512)} %constant.47.clone) | copy-start | bytes 6148
  49.9 15.0 %all-to-all-start.2 = ((bf16[16,72,128]{2,1,0:T(8,128)(2,1)}), bf16[16,72,128]{2,1,0:T(8,128)(2,1)S(1)}, u32[]{:S(2)}, u32[]{:S(2)}) async-start(bf16[16,72,128]{2,1,0:T(8,128)(2,1)} %correlate.1), calls=%async_computation.2 | async-start | bytes 589824 | tf_op jit(solution)/shard_map/all_to_all | solution.py:339

commit v4 on v3

--- a/solution.py
+++ b/solution.py
@@ -79,12 +79,12 @@
 
 def right_product(x, high, low):
     xh, xl = parts2(x)
-    return dot(xh, high) + (dot(xl, high) + dot(xh, low))
+    return dot(jnp.concatenate([xl, xh, xh], axis=1), jnp.concatenate([high, low, high], axis=0))
 
 
 def left_product(high, low, x):
     xh, xl = parts2(x)
-    return dot(high, xh) + (dot(high, xl) + dot(low, xh))
+    return dot(jnp.concatenate([high, low, high], axis=1), jnp.concatenate([xl, xh, xh], axis=0))
 
 
 def whiten_kernel(alive, starts, halves, x_ref, mats, twid_ref, out_ref, spread_ref, sig, pad):
@@ -112,14 +112,14 @@
         col = lax.broadcasted_iota(jnp.int32, (128, 128), 1)
         gap = row - col
         bands = (gap >= 128 - half, jnp.abs(gap) <= half, -gap >= 128 - half)
-        total = None
+        terms, weights = [], []
         signal = jnp.concatenate([pad[pl.ds((r * 2 + s) * 48 + 8, Q), :] for s in range(2)], axis=0)
         for k, band in enumerate(bands):
             weight = jnp.where(band, 1.0, 0.0).astype(bf16)
             value = jnp.concatenate([pad[pl.ds((r * 2 + s) * 48 + 7 + k, Q), :] for s in range(2)], axis=0)
-            for term in parts3(jnp.abs(value)):
-                add = dot(term, weight)
-                total = add if total is None else total + add
+            terms.extend(parts3(jnp.abs(value)))
+            weights.extend([weight] * 3)
+        total = dot(jnp.concatenate(terms, axis=1), jnp.concatenate(weights, axis=0))
         level = total / (2 * half + 1).astype(f32)
         normed.append(signal / (level + TINY))
     x = jnp.concatenate(normed, axis=0)
@@ -135,10 +135,8 @@
     spec = right_product(turned, second_h, second_l)
     square = spec * spec
     size = jnp.sqrt(square + pltpu.roll(square, BINS, 1))
-    sums = None
-    for term in parts3(size):
-        add = dot(mats[2048:2432, :], term)
-        sums = add if sums is None else sums + add
+    tri = mats[2048:2432, :]
+    sums = dot(jnp.concatenate([tri] * 3, axis=1), jnp.concatenate(parts3(size), axis=0))
     smooth = (sums[0:128] + pltpu.roll(sums[128:256], 1, 1) + pltpu.roll(sums[256:384], 127, 1)) / 65.0
     k1 = lax.broadcasted_iota(jnp.int32, (128, 128), 0) % Q
     jj = lax.broadcasted_iota(jnp.int32, (128, 128), 1) % BINS
@@ -181,14 +179,9 @@
     )(alive, starts, halves, x, *consts)
 
 
-def load_lines(refs, line):
-    at = 0
-    for ref in refs:
-        for k in range(ref.shape[0]):
-            line[at:at + 2, 128:128 + LINE] = ref[k]
-            at += 2
-    line[:, 0:128] = line[:, LINE:LINE + 128]
-    line[:, 128 + LINE:256 + LINE] = line[:, 128:256]
+def load_lines(ref, line, first, last, to):
+    for k in range(16):
+        line[2 * k:2 * k + 2, to:to + last - first] = ref[k, :, first:last]
 
 
 def corr_kernel(rows_ref, *rest):
@@ -198,15 +191,22 @@
         copies.append(pltpu.make_async_copy(ref, held.at[at:at + ref.shape[0]], sems.at[k]))
         copies[-1].start()
         at += ref.shape[0]
-    load_lines([rows_ref], xi)
-    for copy in copies:
-        copy.wait()
-    load_lines([held], xj)
     wide = CHUNK + 256
     slots = ((left0, right0), (left1, right1))
 
     def expand(step):
         left, right = slots[step % 2]
+        for ref, line in ((rows_ref, xi), (held, xj)):
+            if step == 0:
+                if ref is held:
+                    for copy in copies:
+                        copy.wait()
+                load_lines(ref, line, LINE - 128, LINE, 0)
+            first = step * CHUNK + 128 if step else 0
+            last = min((step + 1) * CHUNK + 128, LINE)
+            load_lines(ref, line, first, last, 128 + first)
+            if last == LINE:
+                line[:, 128 + LINE:256 + LINE] = line[:, 128:256]
         line_i = xi[:, step * CHUNK:step * CHUNK + wide]
         line_j = xj[:, step * CHUNK:step * CHUNK + wide]
         for a in range(A_BLOCKS + 1):
@@ -320,11 +320,12 @@
     return lax.ppermute(value, ("z", "core"), pairs)
 
 
-def columns_by_hops(pair):
-    one = shed(pair, 1)
-    more = shed(jnp.concatenate([pair, one], axis=0), 2)
+def columns_by_hops(white, other):
+    own_up, other_up = shed(white, 1), shed(other, 1)
+    one = jnp.concatenate([own_up, other_up], axis=0)
+    more = shed(jnp.concatenate([white, other, own_up, other_up], axis=0), 2)
     four = shed(more[2:4], 1)
-    return one, more, four, crossed(one), crossed(more)
+    return white, other, one, more, four, crossed(one), crossed(more)
 
 
 def on_device(raw, alive, seg_start, norm_half):
@@ -334,8 +335,8 @@
     white, spread = whiten(traces, alive, seg_start, norm_half)
     rows = lax.all_to_all(spread, PLANE, split_axis=0, concat_axis=0, tiled=True)
     white = white[None]
-    pair = jnp.concatenate([white, crossed(white)], axis=0)
-    block = correlate(rows, (pair,) + columns_by_hops(pair))
+    other = crossed(white)
+    block = correlate(rows, columns_by_hops(white, other))
     back = lax.all_to_all(block, PLANE, split_axis=0, concat_axis=0, tiled=True)
     k = np.arange(512)
     e, pair_id, side = k // 32, (k // 4) % 8, (k // 2) % 2

time: 66.8 us -> 65.7 us (0.984)
  waiting for transfers between devices: 21.8 us -> 16.8 us
  starting transfers between devices: 17.4 us -> 22.3 us
  other arithmetic: 1.21 us -> 0.4 us
    ppermute x3 -> x4, starting transfers between devices: 4.37 us -> 9.23 us  [shed(): return lax.ppermute(value, ('z', 'core'), pairs)]
    ppermute x3 -> x4, waiting for transfers between devices: 12.4 us -> 9.42 us  [shed(): return lax.ppermute(value, ('z', 'core'), pairs)]
    ppermute x3, waiting for transfers between devices: 1.99 us -> 0.01 us  [crossed(): return lax.ppermute(value, 'core', [(0, 1), (1, 0)])]
    concatenate x2 -> x1, other arithmetic: 1.05 us -> 0.24 us  [columns_by_hops(): more = shed(jnp.concatenate([white, other, own_up, other_up], axis=0), 2)]
  transfers between devices with their start and end apart: 8 -> 9, of which waited for: 6 -> 4; matrix products, arithmetic and copies ran while one was open for 1% -> 1% of each run, Pallas kernels for 0% -> 0%
where the time goes in v4:
time: 65.7 us; the launch traced here: 65.3 us
  starting transfers between devices  22.3 us (34%)
  waiting for transfers between devices  16.8 us (26%)
  blocking collectives  13.6 us (21%)
  Pallas kernels  11 us (17%)
  local copies, waits for them, and re-layouts  1.02 us (2%)
    all_to_all x1, blocking collectives, on_device(): lax.all_to_all(sent, SLABS, split_axis=0, concat_axis=0, tiled=True)  13.6 us
    ppermute x4, waiting for transfers between devices, shed(): return lax.ppermute(value, ('z', 'core'), pairs)  9.42 us
    ppermute x4, starting transfers between devices, shed(): return lax.ppermute(value, ('z', 'core'), pairs)  9.23 us
    all_to_all x1, starting transfers between devices, on_device(): back = lax.all_to_all(block, PLANE, split_axis=0, concat_axis=0, tiled=True)  7.39 us
    all_to_all x1, waiting for transfers between devices, on_device(): back = lax.all_to_all(block, PLANE, split_axis=0, concat_axis=0, tiled=True)  7.38 us
    pallas_call x1, Pallas kernels, correlate(): pl.pallas_call(corr_kernel, out_shape=jax.ShapeDtypeStruct((16, 72, 128),...  5.89 us
    all_to_all x1, starting transfers between devices, on_device(): lax.all_to_all(spread, PLANE, split_axis=0, concat_axis=0, tiled=True)  5 us
    pallas_call x1, Pallas kernels, whiten(): pl.pallas_call(whiten_kernel, out_shape=(jax.ShapeDtypeStruct((2, LINE),...  3.69 us
  transfers between devices with their start and end apart: 9, of which 4 were waited for; matrix products, arithmetic and copies ran while one was open for 1% of the time, Pallas kernels for 0%

profile of v4, /device:TPU:2, one launch (start us, length us, event | category | flops | bytes accessed | tf_op | source)
XLA Modules:
  0.0 65.3 jit_solution(14703511573591338467)
XLA Ops:
  0.0 0.9 %reshape.14 = f32[2,16,2,2,128]{4,3,2,1,0:T(2,128)S(1)} reshape(f32[2,32,256]{2,1,0:T(8,128)} %param.9) | data formatting | bytes 131072 | tf_op jit(solution)/shard_map/reshape | solution.py:333
  0.9 13.6 %all_to_all.15 = f32[16,8,128]{2,1,0:T(8,128)} all-to-all(f32[16,8,128]{2,1,0:T(8,128)S(1)} %bitcast.10), channel_id=1, replica_groups=mesh['z'=8,'yl'=2,'x'=4,'yh'=2,'core'=2] {'x','yh','core'}, dimensions={0} | all-to-all | bytes 131072 | tf_op jit(solution)/shard_map/all_to_all | solution.py:334
  14.5 3.7 %whiten.1 = (bf16[2,8320]{1,0:T(2,128)(2,1)}, bf16[16,2,8320]{2,1,0:T(2,128)(2,1)}) custom-call(s32[2]{0:T(128)} %alive.1, s32[2]{0:T(128)} %starts.1, s32[2]{0:T(128)} %halves.1, f32[128,128]{1,0:T(8,128)} %bitcast.12, bf16[2432,128]{1,0:T(8,128)(2,1)} %constant.45.clone.mats, f32[256,128]{1,0:T(8,128)} %constant.46.clone.twid_ref), custom_call_target="tpu_custom_call" | custom-call | tf_op jit(solution)/shard_map/whiten/pallas_call | solution.py:172
  18.2 0.1 collective-permute-start
  18.3 1.9 %collective-permute-start.1 = (bf16[1,2,8320]{2,1,0:T(2,128)(2,1)}, bf16[1,2,8320]{2,1,0:T(2,128)(2,1)S(1)}, u32[]{:S(2)}, u32[]{:S(2)}) collective-permute-start(bf16[1,2,8320]{2,1,0:T(2,128)(2,1)} %bitcast.7), channel_id=1, source_target_pairs={{0,32},{1,225},{32,64},{33,1},{64,96},{65,33},{96,128},{97,65},{12... | collective-permute-start | bytes 99848 | tf_op jit(solution)/shard_map/ppermute | solution.py:320
  20.3 0.0 collective-permute-done.rest_1_
  20.3 1.9 %collective-permute-start.2 = (bf16[1,2,8320]{2,1,0:T(2,128)(2,1)S(1)}, bf16[1,2,8320]{2,1,0:T(2,128)(2,1)S(1)}, u32[]{:S(2)}, u32[]{:S(2)}) collective-permute-start(bf16[1,2,8320]{2,1,0:T(2,128)(2,1)S(1)} %collective-permute-done.rest_1_), channel_id=1, source_target_pairs={{0,32},{1,225},{32,64},{33,1},{64,96},{65,33},{96,128},{97,65},{12... | collective-permute-start | bytes 99848 | tf_op jit(solution)/shard_map/ppermute | solution.py:320
  22.2 5.0 %all-to-all-start.1 = ((bf16[16,2,8320]{2,1,0:T(2,128)(2,1)}), bf16[16,2,8320]{2,1,0:T(2,128)(2,1)S(1)}, u32[]{:S(2)}, u32[]{:S(2)}) async-start(bf16[16,2,8320]{2,1,0:T(2,128)(2,1)} %get-tuple-element.7), calls=%async_computation.1 | async-start | bytes 1064960 | tf_op jit(solution)/shard_map/all_to_all | solution.py:336
  27.2 0.0 collective-permute-done.1
  27.2 0.2 collective-permute-done.2
  27.4 0.0 copy-done
  27.4 0.2 pad_maximum_fusion
  27.6 4.4 %collective-permute-start.3 = (bf16[4,2,8320]{2,1,0:T(2,128)(2,1)S(1)}, bf16[4,2,8320]{2,1,0:T(2,128)(2,1)S(1)}, u32[]{:S(2)}, u32[]{:S(2)}) collective-permute-start(bf16[4,2,8320]{2,1,0:T(2,128)(2,1)S(1)} %pad_maximum_fusion), channel_id=1, source_target_pairs={{0,64},{1,193},{32,96},{33,225},{64,128},{65,1},{96,160},{97,33},{... | collective-permute-start | bytes 399368 | tf_op jit(solution)/shard_map/ppermute | solution.py:320
  32.0 4.7 %collective-permute-done.3.rest_3_ = bf16[4,2,8320]{2,1,0:T(2,128)(2,1)S(1)} collective-permute-done((bf16[4,2,8320]{2,1,0:T(2,128)(2,1)S(1)}, bf16[4,2,8320]{2,1,0:T(2,128)(2,1)S(1)}, u32[]{:S(2)}, u32[]{:S(2)}) %collective-permute-start.3) | collective-permute-done | bytes 133152 | tf_op jit(solution)/shard_map/ppermute | solution.py:320
  36.7 0.1 collective-permute-start.6
  36.9 0.5 collective-permute-start.5
  37.4 1.0 %collective-permute-start.4 = (bf16[2,2,8320]{2,1,0:T(2,128)(2,1)S(1)}, bf16[2,2,8320]{2,1,0:T(2,128)(2,1)S(1)}, u32[]{:S(2)}, u32[]{:S(2)}) collective-permute-start(bf16[2,2,8320]{2,1,0:T(2,128)(2,1)S(1)} %slice.4), channel_id=1, source_target_pairs={{0,32},{1,225},{32,64},{33,1},{64,96},{65,33},{96,128},{97,65},{12... | collective-permute-start | bytes 199688 | tf_op jit(solution)/shard_map/ppermute | solution.py:320
  38.4 0.0 collective-permute-done.5.rest_5_
  38.4 4.5 %collective-permute-done.4.rest_4_ = bf16[2,2,8320]{2,1,0:T(2,128)(2,1)S(1)} collective-permute-done((bf16[2,2,8320]{2,1,0:T(2,128)(2,1)S(1)}, bf16[2,2,8320]{2,1,0:T(2,128)(2,1)S(1)}, u32[]{:S(2)}, u32[]{:S(2)}) %collective-permute-start.4) | collective-permute-done | bytes 66592 | tf_op jit(solution)/shard_map/ppermute | solution.py:320
  43.0 0.0 collective-permute-done.6.rest_6_
  43.0 0.0 all-to-all-done.1.rows_ref
  43.0 5.9 %correlate.1 = bf16[16,72,128]{2,1,0:T(8,128)(2,1)} custom-call(bf16[16,2,8320]{2,1,0:T(2,128)(2,1)S(1)} %all-to-all-done.1.rows_ref, bf16[1,2,8320]{2,1,0:T(2,128)(2,1)S(1)} %bitcast.9, bf16[1,2,8320]{2,1,0:T(2,128)(2,1)S(1)} %collective-permute-done.rest_1_, bf16[2,2,8320]{2,1,0:T(2,128)(2,1)S(1)} %constant_dynamic-update-slice_fusion.rest_2_, ...), custom_call_target="tpu_custom_call" | custom-call | flops 2453667840 | bytes 4194304 | tf_op jit(solution)/shard_map/correlate/pallas_call | solution.py:244
  48.9 0.0 copy-start.1
  48.9 0.0 copy-start.2
  48.9 0.0 copy-start.3
  48.9 7.4 %all-to-all-start.2 = ((bf16[16,72,128]{2,1,0:T(8,128)(2,1)}), bf16[16,72,128]{2,1,0:T(8,128)(2,1)S(1)}, u32[]{:S(2)}, u32[]{:S(2)}) async-start(bf16[16,72,128]{2,1,0:T(8,128)(2,1)} %correlate.1), calls=%async_computation.2 | async-start | bytes 589824 | tf_op jit(solution)/shard_map/all_to_all | solution.py:340
  56.3 0.0 copy-done.1
  56.3 0.0 copy-done.2
  56.3 0.0 copy-done.3
  56.4 0.2 fusion.perm_ref
  56.5 7.4 %all-to-all-done.2.x_ref = bf16[16,72,128]{2,1,0:T(8,128)(2,1)S(1)} async-done(((bf16[16,72,128]{2,1,0:T(8,128)(2,1)}), bf16[16,72,128]{2,1,0:T(8,128)(2,1)S(1)}, u32[]{:S(2)}, u32[]{:S(2)}) %all-to-all-start.2) | async-done | bytes 294944 | tf_op jit(solution)/shard_map/all_to_all | solution.py:340
  63.9 1.4 %place.1 = bf16[129,2,512]{2,1,0:T(2,128)(2,1)} custom-call(s32[1]{0:T(128)} %bitcast.own, bf16[16,72,128]{2,1,0:T(8,128)(2,1)S(1)} %all-to-all-done.2.x_ref, bf16[512,512]{1,0:T(8,128)(2,1)S(1)} %fusion.perm_ref), custom_call_target="tpu_custom_call" | custom-call | tf_op jit(solution)/shard_map/place/pallas_call | solution.py:296
  (6 shorter events, 0.1 us)
Async XLA Ops:
  18.2 2.0 %collective-permute-start = (bf16[1,2,8320]{2,1,0:T(2,128)(2,1)}, bf16[1,2,8320]{2,1,0:T(2,128)(2,1)S(1)}, u32[]{:S(2)}, u32[]{:S(2)}) collective-permute-start(bf16[1,2,8320]{2,1,0:T(2,128)(2,1)} %bitcast.6), channel_id=1, source_target_pairs={{0,1},{1,0},{2,3},{3,2},{4,5},{5,4},{6,7},{7,6},{8,9},{9,8},{10,11... | collective-permute-start | bytes 99848 | tf_op jit(solution)/shard_map/ppermute | solution.py:312
  18.3 8.9 %collective-permute-start.1 = (bf16[1,2,8320]{2,1,0:T(2,128)(2,1)}, bf16[1,2,8320]{2,1,0:T(2,128)(2,1)S(1)}, u32[]{:S(2)}, u32[]{:S(2)}) collective-permute-start(bf16[1,2,8320]{2,1,0:T(2,128)(2,1)} %bitcast.7), channel_id=1, source_target_pairs={{0,32},{1,225},{32,64},{33,1},{64,96},{65,33},{96,128},{97,65},{12... | collective-permute-start | bytes 99848 | tf_op jit(solution)/shard_map/ppermute | solution.py:320
  20.3 7.1 %collective-permute-start.2 = (bf16[1,2,8320]{2,1,0:T(2,128)(2,1)S(1)}, bf16[1,2,8320]{2,1,0:T(2,128)(2,1)S(1)}, u32[]{:S(2)}, u32[]{:S(2)}) collective-permute-start(bf16[1,2,8320]{2,1,0:T(2,128)(2,1)S(1)} %collective-permute-done.rest_1_), channel_id=1, source_target_pairs={{0,32},{1,225},{32,64},{33,1},{64,96},{65,33},{96,128},{97,65},{12... | collective-permute-start | bytes 99848 | tf_op jit(solution)/shard_map/ppermute | solution.py:320
  22.2 5.2 %copy-start = (bf16[2,8320]{1,0:T(2,128)(2,1)S(1)}, bf16[2,8320]{1,0:T(2,128)(2,1)}, u32[]{:S(2)}) copy-start(bf16[2,8320]{1,0:T(2,128)(2,1)} %get-tuple-element.8) | copy-start | bytes 99844
  22.2 20.8 %all-to-all-start.1 = ((bf16[16,2,8320]{2,1,0:T(2,128)(2,1)}), bf16[16,2,8320]{2,1,0:T(2,128)(2,1)S(1)}, u32[]{:S(2)}, u32[]{:S(2)}) async-start(bf16[16,2,8320]{2,1,0:T(2,128)(2,1)} %get-tuple-element.7), calls=%async_computation.1 | async-start | bytes 1064960 | tf_op jit(solution)/shard_map/all_to_all | solution.py:336
  27.6 9.1 %collective-permute-start.3 = (bf16[4,2,8320]{2,1,0:T(2,128)(2,1)S(1)}, bf16[4,2,8320]{2,1,0:T(2,128)(2,1)S(1)}, u32[]{:S(2)}, u32[]{:S(2)}) collective-permute-start(bf16[4,2,8320]{2,1,0:T(2,128)(2,1)S(1)} %pad_maximum_fusion), channel_id=1, source_target_pairs={{0,64},{1,193},{32,96},{33,225},{64,128},{65,1},{96,160},{97,33},{... | collective-permute-start | bytes 399368 | tf_op jit(solution)/shard_map/ppermute | solution.py:320
  36.7 6.3 %collective-permute-start.6 = (bf16[4,2,8320]{2,1,0:T(2,128)(2,1)S(1)}, bf16[4,2,8320]{2,1,0:T(2,128)(2,1)S(1)}, u32[]{:S(2)}, u32[]{:S(2)}) collective-permute-start(bf16[4,2,8320]{2,1,0:T(2,128)(2,1)S(1)} %collective-permute-done.3.rest_3_), channel_id=1, source_target_pairs={{0,1},{1,0},{2,3},{3,2},{4,5},{5,4},{6,7},{7,6},{8,9},{9,8},{10,11... | collective-permute-start | bytes 399368 | tf_op jit(solution)/shard_map/ppermute | solution.py:312
  36.9 1.5 %collective-permute-start.5 = (bf16[2,2,8320]{2,1,0:T(2,128)(2,1)S(1)}, bf16[2,2,8320]{2,1,0:T(2,128)(2,1)S(1)}, u32[]{:S(2)}, u32[]{:S(2)}) collective-permute-start(bf16[2,2,8320]{2,1,0:T(2,128)(2,1)S(1)} %constant_dynamic-update-slice_fusion.rest_2_), channel_id=1, source_target_pairs={{0,1},{1,0},{2,3},{3,2},{4,5},{5,4},{6,7},{7,6},{8,9},{9,8},{10,11... | collective-permute-start | bytes 199688 | tf_op jit(solution)/shard_map/ppermute | solution.py:312
  37.4 5.6 %collective-permute-start.4 = (bf16[2,2,8320]{2,1,0:T(2,128)(2,1)S(1)}, bf16[2,2,8320]{2,1,0:T(2,128)(2,1)S(1)}, u32[]{:S(2)}, u32[]{:S(2)}) collective-permute-start(bf16[2,2,8320]{2,1,0:T(2,128)(2,1)S(1)} %slice.4), channel_id=1, source_target_pairs={{0,32},{1,225},{32,64},{33,1},{64,96},{65,33},{96,128},{97,65},{12... | collective-permute-start | bytes 199688 | tf_op jit(solution)/shard_map/ppermute | solution.py:320
  48.9 7.4 %copy-start.1 = (s32[512]{0:T(512)S(1)}, s32[512]{0:T(512)}, u32[]{:S(2)}) copy-start(s32[512]{0:T(512)} %constant.49.clone) | copy-start | bytes 6148
  48.9 7.4 %copy-start.2 = (s32[512]{0:T(512)S(1)}, s32[512]{0:T(512)}, u32[]{:S(2)}) copy-start(s32[512]{0:T(512)} %constant.48.clone) | copy-start | bytes 6148
  48.9 7.4 %copy-start.3 = (s32[512]{0:T(512)S(1)}, s32[512]{0:T(512)}, u32[]{:S(2)}) copy-start(s32[512]{0:T(512)} %constant.47.clone) | copy-start | bytes 6148
  48.9 15.0 %all-to-all-start.2 = ((bf16[16,72,128]{2,1,0:T(8,128)(2,1)}), bf16[16,72,128]{2,1,0:T(8,128)(2,1)S(1)}, u32[]{:S(2)}, u32[]{:S(2)}) async-start(bf16[16,72,128]{2,1,0:T(8,128)(2,1)} %correlate.1), calls=%async_computation.2 | async-start | bytes 589824 | tf_op jit(solution)/shard_map/all_to_all | solution.py:340

commit v5 on v4

--- a/solution.py
+++ b/solution.py
@@ -180,6 +180,9 @@
 
 
 def load_lines(ref, line, first, last, to):
+    if len(ref.shape) == 2:
+        line[:, to:to + last - first] = ref[:, first:last]
+        return
     for k in range(16):
         line[2 * k:2 * k + 2, to:to + last - first] = ref[k, :, first:last]
 
@@ -256,7 +259,7 @@
         compiler_params=pltpu.CompilerParams(vmem_limit_bytes=32 << 20),
         cost_estimate=pl.CostEstimate(flops=2 * rows * cols * LINE, bytes_accessed=4 << 20, transcendentals=0),
         name="correlate",
-    )(rows_in, *cols_in)
+    )(rows_in.reshape(32, LINE), *cols_in)
 
 
 def place_kernel(own, x_ref, perm_ref, out_ref, rows, res):

time: 65.7 us -> 65.5 us (level)
  no operation moved by 1% of the time
where the time goes in v5:
time: 65.5 us; the launch traced here: 65.1 us
  starting transfers between devices  22.3 us (34%)
  waiting for transfers between devices  16.6 us (25%)
  blocking collectives  13.6 us (21%)
  Pallas kernels  10.8 us (16%)
  local copies, waits for them, and re-layouts  1.22 us (2%)
    all_to_all x1, blocking collectives, on_device(): lax.all_to_all(sent, SLABS, split_axis=0, concat_axis=0, tiled=True)  13.6 us
    ppermute x4, starting transfers between devices, shed(): return lax.ppermute(value, ('z', 'core'), pairs)  9.23 us
    ppermute x4, waiting for transfers between devices, shed(): return lax.ppermute(value, ('z', 'core'), pairs)  9.21 us
    all_to_all x1, starting transfers between devices, on_device(): back = lax.all_to_all(block, PLANE, split_axis=0, concat_axis=0, tiled=True)  7.39 us
    all_to_all x1, waiting for transfers between devices, on_device(): back = lax.all_to_all(block, PLANE, split_axis=0, concat_axis=0, tiled=True)  7.38 us
    pallas_call x1, Pallas kernels, correlate(): pl.pallas_call(corr_kernel, out_shape=jax.ShapeDtypeStruct((16, 72, 128),...  5.7 us
    all_to_all x1, starting transfers between devices, on_device(): lax.all_to_all(spread, PLANE, split_axis=0, concat_axis=0, tiled=True)  5 us
    pallas_call x1, Pallas kernels, whiten(): pl.pallas_call(whiten_kernel, out_shape=(jax.ShapeDtypeStruct((2, LINE),...  3.69 us
  transfers between devices with their start and end apart: 9, of which 4 were waited for; matrix products, arithmetic and copies ran while one was open for 1% of the time, Pallas kernels for 0%

profile of v5, /device:TPU:2, one launch (start us, length us, event | category | flops | bytes accessed | tf_op | source)
XLA Modules:
  0.0 65.1 jit_solution(5703680344851533046)
XLA Ops:
  0.0 0.9 %reshape.17 = f32[2,16,2,2,128]{4,3,2,1,0:T(2,128)S(1)} reshape(f32[2,32,256]{2,1,0:T(8,128)} %param.9) | data formatting | bytes 131072 | tf_op jit(solution)/shard_map/reshape | solution.py:336
  0.9 13.6 %all_to_all.15 = f32[16,8,128]{2,1,0:T(8,128)} all-to-all(f32[16,8,128]{2,1,0:T(8,128)S(1)} %bitcast.10), channel_id=1, replica_groups=mesh['z'=8,'yl'=2,'x'=4,'yh'=2,'core'=2] {'x','yh','core'}, dimensions={0} | all-to-all | bytes 131072 | tf_op jit(solution)/shard_map/all_to_all | solution.py:337
  14.5 3.7 %whiten.1 = (bf16[2,8320]{1,0:T(2,128)(2,1)}, bf16[16,2,8320]{2,1,0:T(2,128)(2,1)}) custom-call(s32[2]{0:T(128)} %alive.1, s32[2]{0:T(128)} %starts.1, s32[2]{0:T(128)} %halves.1, f32[128,128]{1,0:T(8,128)} %bitcast.12, bf16[2432,128]{1,0:T(8,128)(2,1)} %constant.45.clone.mats, f32[256,128]{1,0:T(8,128)} %constant.46.clone.twid_ref), custom_call_target="tpu_custom_call" | custom-call | tf_op jit(solution)/shard_map/whiten/pallas_call | solution.py:172
  18.2 0.1 collective-permute-start
  18.3 1.9 %collective-permute-start.1 = (bf16[1,2,8320]{2,1,0:T(2,128)(2,1)}, bf16[1,2,8320]{2,1,0:T(2,128)(2,1)S(1)}, u32[]{:S(2)}, u32[]{:S(2)}) collective-permute-start(bf16[1,2,8320]{2,1,0:T(2,128)(2,1)} %bitcast.7), channel_id=1, source_target_pairs={{0,32},{1,225},{32,64},{33,1},{64,96},{65,33},{96,128},{97,65},{12... | collective-permute-start | bytes 99848 | tf_op jit(solution)/shard_map/ppermute | solution.py:323
  20.3 0.0 collective-permute-done.rest_1_
  20.3 1.9 %collective-permute-start.2 = (bf16[1,2,8320]{2,1,0:T(2,128)(2,1)S(1)}, bf16[1,2,8320]{2,1,0:T(2,128)(2,1)S(1)}, u32[]{:S(2)}, u32[]{:S(2)}) collective-permute-start(bf16[1,2,8320]{2,1,0:T(2,128)(2,1)S(1)} %collective-permute-done.rest_1_), channel_id=1, source_target_pairs={{0,32},{1,225},{32,64},{33,1},{64,96},{65,33},{96,128},{97,65},{12... | collective-permute-start | bytes 99848 | tf_op jit(solution)/shard_map/ppermute | solution.py:323
  22.2 5.0 %all-to-all-start.1 = ((bf16[16,2,8320]{2,1,0:T(2,128)(2,1)}), bf16[16,2,8320]{2,1,0:T(2,128)(2,1)S(1)}, u32[]{:S(2)}, u32[]{:S(2)}) async-start(bf16[16,2,8320]{2,1,0:T(2,128)(2,1)} %get-tuple-element.7), calls=%async_computation.1 | async-start | bytes 1064960 | tf_op jit(solution)/shard_map/all_to_all | solution.py:339
  27.2 0.0 collective-permute-done.1
  27.2 0.2 collective-permute-done.2
  27.4 0.0 copy-done
  27.4 0.2 pad_maximum_fusion
  27.6 4.4 %collective-permute-start.3 = (bf16[4,2,8320]{2,1,0:T(2,128)(2,1)S(1)}, bf16[4,2,8320]{2,1,0:T(2,128)(2,1)S(1)}, u32[]{:S(2)}, u32[]{:S(2)}) collective-permute-start(bf16[4,2,8320]{2,1,0:T(2,128)(2,1)S(1)} %pad_maximum_fusion), channel_id=1, source_target_pairs={{0,64},{1,193},{32,96},{33,225},{64,128},{65,1},{96,160},{97,33},{... | collective-permute-start | bytes 399368 | tf_op jit(solution)/shard_map/ppermute | solution.py:323
  32.0 4.7 %collective-permute-done.3.rest_3_ = bf16[4,2,8320]{2,1,0:T(2,128)(2,1)S(1)} collective-permute-done((bf16[4,2,8320]{2,1,0:T(2,128)(2,1)S(1)}, bf16[4,2,8320]{2,1,0:T(2,128)(2,1)S(1)}, u32[]{:S(2)}, u32[]{:S(2)}) %collective-permute-start.3) | collective-permute-done | bytes 133152 | tf_op jit(solution)/shard_map/ppermute | solution.py:323
  36.7 0.1 collective-permute-start.6
  36.9 0.5 collective-permute-start.5
  37.4 1.0 %collective-permute-start.4 = (bf16[2,2,8320]{2,1,0:T(2,128)(2,1)S(1)}, bf16[2,2,8320]{2,1,0:T(2,128)(2,1)S(1)}, u32[]{:S(2)}, u32[]{:S(2)}) collective-permute-start(bf16[2,2,8320]{2,1,0:T(2,128)(2,1)S(1)} %slice.4), channel_id=1, source_target_pairs={{0,32},{1,225},{32,64},{33,1},{64,96},{65,33},{96,128},{97,65},{12... | collective-permute-start | bytes 199688 | tf_op jit(solution)/shard_map/ppermute | solution.py:323
  38.4 0.0 all-to-all-done.1
  38.4 0.2 reshape.20.rows_ref
  38.6 0.0 collective-permute-done.5.rest_5_
  38.6 4.3 %collective-permute-done.4.rest_4_ = bf16[2,2,8320]{2,1,0:T(2,128)(2,1)S(1)} collective-permute-done((bf16[2,2,8320]{2,1,0:T(2,128)(2,1)S(1)}, bf16[2,2,8320]{2,1,0:T(2,128)(2,1)S(1)}, u32[]{:S(2)}, u32[]{:S(2)}) %collective-permute-start.4) | collective-permute-done | bytes 66592 | tf_op jit(solution)/shard_map/ppermute | solution.py:323
  43.0 0.0 collective-permute-done.6.rest_6_
  43.0 5.7 %correlate.1 = bf16[16,72,128]{2,1,0:T(8,128)(2,1)} custom-call(bf16[32,8320]{1,0:T(8,128)(2,1)S(1)} %reshape.20.rows_ref, bf16[1,2,8320]{2,1,0:T(2,128)(2,1)S(1)} %bitcast.9, bf16[1,2,8320]{2,1,0:T(2,128)(2,1)S(1)} %collective-permute-done.rest_1_, bf16[2,2,8320]{2,1,0:T(2,128)(2,1)S(1)} %constant_dynamic-update-slice_fusion.rest_2_, ...), custom_call_target="tpu_custom_call" | custom-call | flops 2453667840 | bytes 4194304 | tf_op jit(solution)/shard_map/correlate/pallas_call | solution.py:247
  48.7 0.0 copy-start.1
  48.7 0.0 copy-start.2
  48.7 0.0 copy-start.3
  48.7 7.4 %all-to-all-start.2 = ((bf16[16,72,128]{2,1,0:T(8,128)(2,1)}), bf16[16,72,128]{2,1,0:T(8,128)(2,1)S(1)}, u32[]{:S(2)}, u32[]{:S(2)}) async-start(bf16[16,72,128]{2,1,0:T(8,128)(2,1)} %correlate.1), calls=%async_computation.2 | async-start | bytes 589824 | tf_op jit(solution)/shard_map/all_to_all | solution.py:343
  56.1 0.0 copy-done.2
  56.1 0.0 copy-done.3
  56.2 0.2 fusion.perm_ref
  56.3 7.4 %all-to-all-done.2.x_ref = bf16[16,72,128]{2,1,0:T(8,128)(2,1)S(1)} async-done(((bf16[16,72,128]{2,1,0:T(8,128)(2,1)}), bf16[16,72,128]{2,1,0:T(8,128)(2,1)S(1)}, u32[]{:S(2)}, u32[]{:S(2)}) %all-to-all-start.2) | async-done | bytes 294944 | tf_op jit(solution)/shard_map/all_to_all | solution.py:343
  63.7 1.4 %place.1 = bf16[129,2,512]{2,1,0:T(2,128)(2,1)} custom-call(s32[1]{0:T(128)} %bitcast.own, bf16[16,72,128]{2,1,0:T(8,128)(2,1)S(1)} %all-to-all-done.2.x_ref, bf16[512,512]{1,0:T(8,128)(2,1)S(1)} %fusion.perm_ref), custom_call_target="tpu_custom_call" | custom-call | tf_op jit(solution)/shard_map/place/pallas_call | solution.py:299
  (7 shorter events, 0.1 us)
Async XLA Ops:
  18.2 2.0 %collective-permute-start = (bf16[1,2,8320]{2,1,0:T(2,128)(2,1)}, bf16[1,2,8320]{2,1,0:T(2,128)(2,1)S(1)}, u32[]{:S(2)}, u32[]{:S(2)}) collective-permute-start(bf16[1,2,8320]{2,1,0:T(2,128)(2,1)} %bitcast.6), channel_id=1, source_target_pairs={{0,1},{1,0},{2,3},{3,2},{4,5},{5,4},{6,7},{7,6},{8,9},{9,8},{10,11... | collective-permute-start | bytes 99848 | tf_op jit(solution)/shard_map/ppermute | solution.py:315
  18.3 8.9 %collective-permute-start.1 = (bf16[1,2,8320]{2,1,0:T(2,128)(2,1)}, bf16[1,2,8320]{2,1,0:T(2,128)(2,1)S(1)}, u32[]{:S(2)}, u32[]{:S(2)}) collective-permute-start(bf16[1,2,8320]{2,1,0:T(2,128)(2,1)} %bitcast.7), channel_id=1, source_target_pairs={{0,32},{1,225},{32,64},{33,1},{64,96},{65,33},{96,128},{97,65},{12... | collective-permute-start | bytes 99848 | tf_op jit(solution)/shard_map/ppermute | solution.py:323
  20.3 7.1 %collective-permute-start.2 = (bf16[1,2,8320]{2,1,0:T(2,128)(2,1)S(1)}, bf16[1,2,8320]{2,1,0:T(2,128)(2,1)S(1)}, u32[]{:S(2)}, u32[]{:S(2)}) collective-permute-start(bf16[1,2,8320]{2,1,0:T(2,128)(2,1)S(1)} %collective-permute-done.rest_1_), channel_id=1, source_target_pairs={{0,32},{1,225},{32,64},{33,1},{64,96},{65,33},{96,128},{97,65},{12... | collective-permute-start | bytes 99848 | tf_op jit(solution)/shard_map/ppermute | solution.py:323
  22.2 5.2 %copy-start = (bf16[2,8320]{1,0:T(2,128)(2,1)S(1)}, bf16[2,8320]{1,0:T(2,128)(2,1)}, u32[]{:S(2)}) copy-start(bf16[2,8320]{1,0:T(2,128)(2,1)} %get-tuple-element.8) | copy-start | bytes 99844
  22.2 16.2 %all-to-all-start.1 = ((bf16[16,2,8320]{2,1,0:T(2,128)(2,1)}), bf16[16,2,8320]{2,1,0:T(2,128)(2,1)S(1)}, u32[]{:S(2)}, u32[]{:S(2)}) async-start(bf16[16,2,8320]{2,1,0:T(2,128)(2,1)} %get-tuple-element.7), calls=%async_computation.1 | async-start | bytes 1064960 | tf_op jit(solution)/shard_map/all_to_all | solution.py:339
  27.6 9.1 %collective-permute-start.3 = (bf16[4,2,8320]{2,1,0:T(2,128)(2,1)S(1)}, bf16[4,2,8320]{2,1,0:T(2,128)(2,1)S(1)}, u32[]{:S(2)}, u32[]{:S(2)}) collective-permute-start(bf16[4,2,8320]{2,1,0:T(2,128)(2,1)S(1)} %pad_maximum_fusion), channel_id=1, source_target_pairs={{0,64},{1,193},{32,96},{33,225},{64,128},{65,1},{96,160},{97,33},{... | collective-permute-start | bytes 399368 | tf_op jit(solution)/shard_map/ppermute | solution.py:323
  36.7 6.3 %collective-permute-start.6 = (bf16[4,2,8320]{2,1,0:T(2,128)(2,1)S(1)}, bf16[4,2,8320]{2,1,0:T(2,128)(2,1)S(1)}, u32[]{:S(2)}, u32[]{:S(2)}) collective-permute-start(bf16[4,2,8320]{2,1,0:T(2,128)(2,1)S(1)} %collective-permute-done.3.rest_3_), channel_id=1, source_target_pairs={{0,1},{1,0},{2,3},{3,2},{4,5},{5,4},{6,7},{7,6},{8,9},{9,8},{10,11... | collective-permute-start | bytes 399368 | tf_op jit(solution)/shard_map/ppermute | solution.py:315
  36.9 1.8 %collective-permute-start.5 = (bf16[2,2,8320]{2,1,0:T(2,128)(2,1)S(1)}, bf16[2,2,8320]{2,1,0:T(2,128)(2,1)S(1)}, u32[]{:S(2)}, u32[]{:S(2)}) collective-permute-start(bf16[2,2,8320]{2,1,0:T(2,128)(2,1)S(1)} %constant_dynamic-update-slice_fusion.rest_2_), channel_id=1, source_target_pairs={{0,1},{1,0},{2,3},{3,2},{4,5},{5,4},{6,7},{7,6},{8,9},{9,8},{10,11... | collective-permute-start | bytes 199688 | tf_op jit(solution)/shard_map/ppermute | solution.py:315
  37.4 5.6 %collective-permute-start.4 = (bf16[2,2,8320]{2,1,0:T(2,128)(2,1)S(1)}, bf16[2,2,8320]{2,1,0:T(2,128)(2,1)S(1)}, u32[]{:S(2)}, u32[]{:S(2)}) collective-permute-start(bf16[2,2,8320]{2,1,0:T(2,128)(2,1)S(1)} %slice.4), channel_id=1, source_target_pairs={{0,32},{1,225},{32,64},{33,1},{64,96},{65,33},{96,128},{97,65},{12... | collective-permute-start | bytes 199688 | tf_op jit(solution)/shard_map/ppermute | solution.py:323
  48.7 7.4 %copy-start.1 = (s32[512]{0:T(512)S(1)}, s32[512]{0:T(512)}, u32[]{:S(2)}) copy-start(s32[512]{0:T(512)} %constant.49.clone) | copy-start | bytes 6148
  48.7 7.4 %copy-start.2 = (s32[512]{0:T(512)S(1)}, s32[512]{0:T(512)}, u32[]{:S(2)}) copy-start(s32[512]{0:T(512)} %constant.48.clone) | copy-start | bytes 6148
  48.7 7.4 %copy-start.3 = (s32[512]{0:T(512)S(1)}, s32[512]{0:T(512)}, u32[]{:S(2)}) copy-start(s32[512]{0:T(512)} %constant.47.clone) | copy-start | bytes 6148
  48.7 15.0 %all-to-all-start.2 = ((bf16[16,72,128]{2,1,0:T(8,128)(2,1)}), bf16[16,72,128]{2,1,0:T(8,128)(2,1)S(1)}, u32[]{:S(2)}, u32[]{:S(2)}) async-start(bf16[16,72,128]{2,1,0:T(8,128)(2,1)} %correlate.1), calls=%async_computation.2 | async-start | bytes 589824 | tf_op jit(solution)/shard_map/all_to_all | solution.py:343
